TPU v7x, 128 devices: a whole 4x4x4 slice. The times are simulated.
128 devices in a mesh: facet: 8 (over y, core), sub: 16 (over z, x).
Axes of the slice: x: 4, y: 4, z: 4, core: 2. Of those that a mesh axis runs over, the one named last changes fastest.
Arguments:
- facet_data: bfloat16 [2, 16, 65536], P(None, None, ('facet', 'sub')), may hold values from -6 to 6
- subgrid_pos: int32 [128], P(('facet', 'sub')), may hold values from 0 to 65408, as said below
- vis_counts: int32 [128], P(('facet', 'sub')), may hold values from 128 to 512, as said below
- vis_u_fine: int32 [128, 512], P(('facet', 'sub')), may hold values from 0 to 8079
- vis_v_fine: int32 [128, 512], P(('facet', 'sub')), may hold values from 0 to 143
- vis_observed: float32 [2, 128, 512], P(None, ('facet', 'sub')), may hold values from -6 to 6
Outputs:
- vis_residual: float32 [2, 128, 512], P(None, ('facet', 'sub'))
- facet_residual: float32 [2, 16, 65536], P(None, None, ('facet', 'sub'))
Inputs may be any that keep to these rules, and one draw needn't show every extreme that they name: `subgrid_pos`: distinct multiples of 128; a subgrid's u cells o to o + 511 are taken modulo 65536. The first vis_counts[s] slots of subgrid s are live; some subgrid has all 512 slots live.
All inputs are finite; a program needn't handle non-finite values.
Results may differ from a plain program's by a relative error of at most 0.012.
Values may be sent and summed in bfloat16 or wider, within the bound.
No kernel may reach another device: no remote copies, remote signals or barrier semaphores. Data moves between devices by JAX's collectives and lax.ppermute only.
A program may use at most 64 MiB of HBM per device.

v0:
```python
import math

import jax
import jax.numpy as jnp
import numpy as np
from jax import lax
from jax.experimental import pallas as pl
from jax.experimental.pallas import tpu as pltpu
from jax.sharding import PartitionSpec as P

SG = 512
KS = 8
OVER = 16
RES = 128
KB = SG // RES
BATCH = 2
ROWS = 8
BF = jnp.bfloat16
F32 = jnp.float32


def split(value):
    high = lax.reduce_precision(value, 8, 7)
    return high.astype(BF), (value - high).astype(BF)


def gather_by_exchange(value, axis):
    count = lax.axis_size(axis)
    copies = jnp.broadcast_to(value[None], (count,) + value.shape)
    return lax.all_to_all(copies, axis, 0, 0, tiled=True)


def block_tables(facets, subs):
    block = np.arange(facets * subs).reshape(facets, subs)
    turn = (np.arange(RES)[None, :, None] * block[:, None, :]) % RES
    angle = turn * (2.0 * math.pi / RES)
    cos, sin = np.cos(angle), np.sin(angle)
    top = np.stack([cos, sin], -1)
    low = np.stack([-sin, cos], -1)
    table = np.concatenate([top, low], 1).reshape(facets, 2 * RES, 2 * subs)
    return table.astype(np.float32)


def host_split(table):
    high = table.astype(jnp.bfloat16)
    return high, (table - high.astype(np.float32)).astype(jnp.bfloat16)


def weights(fine_index, cells):
    middle = fine_index / OVER + (KS - 1) / 2.0
    cell = jnp.floor(fine_index / OVER)
    row = lax.broadcasted_iota(jnp.int32, (cells, fine_index.shape[1]), 0).astype(F32)
    distance = (row - middle) / 0.6
    weight = jnp.exp(-0.5 * (distance * distance))
    return jnp.where((row >= cell) & (row < cell + KS), weight, F32(0.0))


def weight_rows(fine_index, cells):
    cell = jnp.floor(fine_index / OVER)
    tile = jnp.floor(cell / KS)
    inner = cell - tile * KS
    row = lax.broadcasted_iota(jnp.int32, (KS, fine_index.shape[1]), 0).astype(F32)
    wrapped = row < inner
    offset = row - inner + jnp.where(wrapped, F32(KS), F32(0.0))
    distance = (offset - ((KS - 1) / 2.0 + (fine_index / OVER - cell))) / 0.6
    weight = jnp.exp(-0.5 * (distance * distance))
    tile = tile + jnp.where(wrapped, F32(1.0), F32(0.0))
    return [jnp.where(tile == F32(n), weight, F32(0.0)) for n in range(cells // KS)]


def dot(left, right, dims):
    return lax.dot_general(left, right, (dims, ((), ())), preferred_element_type=F32)


def expand(wu_ref, fine_index):
    rows = weight_rows(fine_index, wu_ref.shape[0])
    for n in range(0, len(rows), 2):
        wu_ref[n * KS : (n + 2) * KS, :] = jnp.concatenate(rows[n : n + 2], 0).astype(BF)


def forward_kernel(at_ref, y_ref, d_ref, tc_ref, ts_ref, e_ref, *refs):
    meta_refs = refs[:-4]
    part_ref, ys_ref, gs_ref, wu_ref = refs[-4:]
    groups = len(meta_refs)
    d_table = d_ref[at_ref[0]]
    pieces = y_ref.shape[0]
    half = e_ref.shape[0] // 2
    band = half // KB
    rows_v = gs_ref.shape[1] // band
    lines = pieces // rows_v
    for k in range(KB):
        ys_ref[k] = y_ref[:, k * RES : (k + 1) * RES].astype(F32)
    for v in range(rows_v):
        row = [ys_ref[k, pl.ds(v, lines, stride=rows_v), :] for k in range(KB)]
        row = jnp.concatenate(row, 1).astype(BF)
        spread = dot(d_table, jnp.concatenate([row, row], 0), ((1,), (0,)))
        real_g, imag_g = spread[:RES], spread[RES:]
        cos, sin = tc_ref[...], ts_ref[...]
        real_h = (real_g * cos + imag_g * sin).astype(BF)
        imag_h = (imag_g * cos - real_g * sin).astype(BF)
        share = dot(e_ref[...], jnp.concatenate([real_h, imag_h], 1), ((1,), (1,)))
        share = share[:half] + share[half:]
        for k in range(KB):
            gs_ref[k, pl.ds(v, band, stride=rows_v), :] = share[k * band : (k + 1) * band]
    for s in range(groups):
        grid = [gs_ref[k, s * 2 * rows_v : (s + 1) * 2 * rows_v, :] for k in range(KB)]
        grid = jnp.concatenate(grid, 1)
        high = grid.astype(BF)
        low = (grid - high.astype(F32)).astype(BF)
        expand(wu_ref.at[s], meta_refs[s][0:1, :])
        along = dot(jnp.concatenate([high, low], 0), wu_ref[s], ((1,), (0,)))
        along = along[: 2 * rows_v] + along[2 * rows_v :]
        wv = weights(meta_refs[s][1:2, :], rows_v)
        real = jnp.sum(along[:rows_v] * wv, 0, keepdims=True)
        imag = jnp.sum(along[rows_v:] * wv, 0, keepdims=True)
        place = (at_ref[0] - s) & (groups - 1)
        both = jnp.concatenate([real, imag], 0).astype(BF)
        for n in range(groups):
            part_ref[n, place] = both


def backward_kernel(at_ref, part_ref, e_ref, tc_ref, ts_ref, d_ref, *refs):
    meta_refs = refs[:-6]
    res_ref, out_ref, pred_ref, rs_ref, im_ref, wu_ref = refs[-6:]
    groups = len(meta_refs)
    slots = res_ref.shape[1]
    d_table = d_ref[at_ref[0]]
    lines = d_table.shape[0]
    band = 2 * groups
    rows_v = rs_ref.shape[1] // band
    pred_ref[...] = jnp.sum(part_ref[...].astype(F32), 0)
    slot = lax.broadcasted_iota(jnp.int32, (2, slots), 1).astype(F32)
    for s in range(groups):
        place = (at_ref[0] - s) & (groups - 1)
        meta = meta_refs[s]
        seen = meta[2:4, :] - pred_ref[place]
        residual = jnp.where(slot < meta[5:6, :], seen, F32(0.0))
        if s == 0:
            res_ref[...] = residual
        wv = weights(meta[1:2, :], rows_v)
        spread = jnp.concatenate([wv * residual[0:1], wv * residual[1:2]], 0).astype(BF)
        expand(wu_ref.at[s], meta[0:1, :])
        cells = dot(spread, wu_ref[s], ((1,), (1,)))
        for k in range(KB):
            rs_ref[k, s * 2 * rows_v : (s + 1) * 2 * rows_v, :] = cells[:, k * RES : (k + 1) * RES]
    e_table = e_ref[: KB * band, :]
    for v in range(0, rows_v, BATCH):
        cells = []
        for n in range(BATCH):
            rows = [rs_ref[k, pl.ds(v + n, band, stride=rows_v), :] for k in range(KB)]
            cells.append(jnp.concatenate(rows, 0))
        cells = jnp.concatenate(cells, 1).astype(BF)
        back = dot(cells, e_table, ((0,), (0,)))
        for n in range(BATCH):
            real_b, imag_b = jnp.split(back[n * RES : (n + 1) * RES], 2, 1)
            cos, sin = tc_ref[...], ts_ref[...]
            real_m = (real_b * cos - imag_b * sin).astype(BF)
            imag_m = (imag_b * cos + real_b * sin).astype(BF)
            image = dot(d_table, jnp.concatenate([real_m, imag_m], 0), ((1,), (0,)))
            for k in range(KB):
                im_ref[k, pl.ds(v + n, lines, stride=rows_v), :] = image[
                    :, k * RES : (k + 1) * RES
                ]
    for k in range(KB):
        out_ref[:, k * RES : (k + 1) * RES] = im_ref[k].astype(BF)


def shards(facet_data, subgrid_pos, vis_counts, vis_u_fine, vis_v_fine, vis_observed):
    facets = lax.axis_size("facet")
    subs = lax.axis_size("sub")
    rows_v = facet_data.shape[1]
    slots = vis_u_fine.shape[1]
    facet = lax.axis_index("facet")
    inside = jnp.arange(SG, dtype=jnp.int32)

    gathered = gather_by_exchange(facet_data, "sub")

    def wide(value):
        return jnp.broadcast_to(value.astype(F32)[:, None], (1, slots))

    meta = jnp.concatenate(
        [
            vis_u_fine.astype(F32),
            vis_v_fine.astype(F32),
            vis_observed[0],
            vis_observed[1],
            wide(subgrid_pos // RES),
            wide(vis_counts),
            jnp.zeros((ROWS - 6, slots), F32),
        ],
        0,
    )
    metas = [meta]
    for d in range(1, facets):
        ring = [(n, (n + d) % facets) for n in range(facets)]
        metas.append(lax.ppermute(meta, "facet", ring))

    table = block_tables(facets, subs)
    high_d, low_d = host_split(table)
    into = jnp.asarray(np.concatenate([high_d, low_d], 2))
    outof = jnp.asarray(high_d.transpose(0, 2, 1))
    turn = np.arange(RES)[:, None] * np.arange(SG)[None, :] * (2.0 * math.pi / 65536)
    tw_cos = jnp.asarray(np.cos(turn).astype(np.float32))
    tw_sin = jnp.asarray(np.sin(turn).astype(np.float32))
    spot = jnp.concatenate([m[4:5] for m in metas], 0).astype(jnp.int32)
    step = spot[None] + jnp.arange(KB, dtype=jnp.int32)[:, None, None]
    turn = (step * inside).reshape(KB * facets, SG) % SG
    angle = turn.astype(F32) * (2.0 * math.pi / SG)
    scale = F32(1.0 / 256.0)
    cos, sin = jnp.cos(angle) * scale, jnp.sin(angle) * scale
    lines = jnp.stack(
        [jnp.concatenate([cos, sin], 1), jnp.concatenate([-sin, cos], 1)], 1
    ).reshape(2 * KB * facets, 2 * SG)
    high_e, low_e = split(lines)
    e_table = jnp.concatenate([high_e, low_e], 0)

    at = facet.astype(jnp.int32)[None]
    params = pltpu.CompilerParams(vmem_limit_bytes=24 * 1024 * 1024)
    vmem = pl.BlockSpec(memory_space=pltpu.VMEM)
    smem = pl.BlockSpec(memory_space=pltpu.SMEM)
    part = pl.pallas_call(
        forward_kernel,
        out_shape=jax.ShapeDtypeStruct((facets, facets, 2, slots), BF),
        in_specs=[smem] + [vmem] * (5 + facets),
        scratch_shapes=[
            pltpu.VMEM((KB, 2 * subs * rows_v, RES), F32),
            pltpu.VMEM((KB, 2 * facets * rows_v, RES), F32),
            pltpu.VMEM((facets, SG, slots), BF),
        ],
        compiler_params=params,
        name="forward_share",
    )(
        at, gathered.reshape(2 * subs * rows_v, SG), into, tw_cos, tw_sin, e_table,
        *metas,
    )

    parts = lax.all_to_all(part, "facet", 0, 0, tiled=True)

    residual, image = pl.pallas_call(
        backward_kernel,
        out_shape=(
            jax.ShapeDtypeStruct((2, slots), F32),
            jax.ShapeDtypeStruct((2 * subs * rows_v, SG), BF),
        ),
        in_specs=[smem] + [vmem] * (5 + facets),
        scratch_shapes=[
            pltpu.VMEM((facets, 2, slots), F32),
            pltpu.VMEM((KB, 2 * facets * rows_v, RES), F32),
            pltpu.VMEM((KB, 2 * subs * rows_v, RES), F32),
            pltpu.VMEM((facets, SG, slots), BF),
        ],
        compiler_params=params,
        name="backward_share",
    )(at, parts, e_table, tw_cos, tw_sin, outof, *metas)

    image = image.reshape(subs, 2, rows_v, SG)
    image = lax.all_to_all(image, "sub", 0, 0, tiled=True)
    return (residual[:, None], jnp.sum(image.astype(F32), 0))


def solution(mesh):
    return jax.shard_map(
        shards,
        mesh=mesh,
        in_specs=(
            P(None, None, ("facet", "sub")),
            P(("facet", "sub")),
            P(("facet", "sub")),
            P(("facet", "sub"), None),
            P(("facet", "sub"), None),
            P(None, ("facet", "sub"), None),
        ),
        out_specs=(P(None, ("facet", "sub"), None), P(None, None, ("facet", "sub"))),
        check_vma=False,
    )
```

profile of v0, /device:TPU:1, one launch (start us, length us, event | category | flops | bytes accessed | tf_op | source)
XLA Modules:
  0.0 67.0 jit_solution(17308619032295648877)
XLA Ops:
  1.3 0.7 copy-done.6
  2.0 0.7 copy-done.5
  3.4 2.7 %collective-permute-start = (f32[8,512]{1,0:T(8,128)S(1)}, f32[8,512]{1,0:T(8,128)S(1)}, u32[]{:S(2)}, u32[]{:S(2)}) collective-permute-start(f32[8,512]{1,0:T(8,128)S(1)} %concatenate.19.refs_0_), channel_id=1, source_target_pairs={{0,16},{16,32},{32,48},{48,64},{64,80},{80,96},{96,112},{112,0},{1... | collective-permute-start | bytes 49160 | tf_op jit(solution)/shard_map/ppermute | solution.py:196
  6.1 1.3 %collective-permute-start.1 = (f32[8,512]{1,0:T(8,128)S(1)}, f32[8,512]{1,0:T(8,128)S(1)}, u32[]{:S(2)}, u32[]{:S(2)}) collective-permute-start(f32[8,512]{1,0:T(8,128)S(1)} %concatenate.19.refs_0_), channel_id=1, source_target_pairs={{0,32},{16,48},{32,64},{48,80},{64,96},{80,112},{96,0},{112,16},{1... | collective-permute-start | bytes 49160 | tf_op jit(solution)/shard_map/ppermute | solution.py:196
  7.4 1.7 %collective-permute-start.2 = (f32[8,512]{1,0:T(8,128)S(1)}, f32[8,512]{1,0:T(8,128)S(1)}, u32[]{:S(2)}, u32[]{:S(2)}) collective-permute-start(f32[8,512]{1,0:T(8,128)S(1)} %concatenate.19.refs_0_), channel_id=1, source_target_pairs={{0,48},{16,64},{32,80},{48,96},{64,112},{80,0},{96,16},{112,32},{1... | collective-permute-start | bytes 49160 | tf_op jit(solution)/shard_map/ppermute | solution.py:196
  9.1 0.3 collective-permute-start.3
  9.4 1.9 %collective-permute-start.4 = (f32[8,512]{1,0:T(8,128)S(1)}, f32[8,512]{1,0:T(8,128)S(1)}, u32[]{:S(2)}, u32[]{:S(2)}) collective-permute-start(f32[8,512]{1,0:T(8,128)S(1)} %concatenate.19.refs_0_), channel_id=1, source_target_pairs={{0,80},{16,96},{32,112},{48,0},{64,16},{80,32},{96,48},{112,64},{1... | collective-permute-start | bytes 49160 | tf_op jit(solution)/shard_map/ppermute | solution.py:196
  11.3 0.9 %collective-permute-start.5 = (f32[8,512]{1,0:T(8,128)S(1)}, f32[8,512]{1,0:T(8,128)S(1)}, u32[]{:S(2)}, u32[]{:S(2)}) collective-permute-start(f32[8,512]{1,0:T(8,128)S(1)} %concatenate.19.refs_0_), channel_id=1, source_target_pairs={{0,96},{16,112},{32,0},{48,16},{64,32},{80,48},{96,64},{112,80},{1... | collective-permute-start | bytes 49160 | tf_op jit(solution)/shard_map/ppermute | solution.py:196
  12.2 1.6 %collective-permute-start.6 = (f32[8,512]{1,0:T(8,128)S(1)}, f32[8,512]{1,0:T(8,128)S(1)}, u32[]{:S(2)}, u32[]{:S(2)}) collective-permute-start(f32[8,512]{1,0:T(8,128)S(1)} %concatenate.19.refs_0_), channel_id=1, source_target_pairs={{0,112},{16,0},{32,16},{48,32},{64,48},{80,64},{96,80},{112,96},{1... | collective-permute-start | bytes 49160 | tf_op jit(solution)/shard_map/ppermute | solution.py:196
  13.8 0.9 %broadcast_in_dim.17 = bf16[16,2,16,512]{3,2,1,0:T(8,128)(2,1)} broadcast(bf16[2,16,512]{2,1,0:T(8,128)(2,1)S(1)} %copy-done.4), dimensions={1,2,3} | broadcast | bytes 557056 | tf_op jit(solution)/shard_map/broadcast_in_dim | solution.py:29
  14.7 7.6 %all-to-all-start = ((bf16[16,2,16,512]{3,2,1,0:T(8,128)(2,1)}), bf16[16,2,16,512]{3,2,1,0:T(8,128)(2,1)S(1)}, u32[]{:S(2)}, u32[]{:S(2)}) async-start(bf16[16,2,16,512]{3,2,1,0:T(8,128)(2,1)} %broadcast_in_dim.17), calls=%async_computation | async-start | bytes 1048576 | tf_op jit(solution)/shard_map/all_to_all | solution.py:30
  22.5 0.4 sine_multiply_fusion
  22.9 0.1 stack.10
  23.0 0.1 copy.12
  23.2 0.2 pad_maximum_fusion
  23.4 0.2 reshape.82
  23.7 9.6 %all-to-all-done = bf16[16,2,16,512]{3,2,1,0:T(8,128)(2,1)S(1)} async-done(((bf16[16,2,16,512]{3,2,1,0:T(8,128)(2,1)}), bf16[16,2,16,512]{3,2,1,0:T(8,128)(2,1)S(1)}, u32[]{:S(2)}, u32[]{:S(2)}) %all-to-all-start) | async-done | bytes 524320 | tf_op jit(solution)/shard_map/all_to_all | solution.py:30
  33.3 3.7 %forward_share.1 = bf16[8,8,2,512]{3,2,1,0:T(2,128)(2,1)S(1)} custom-call(s32[1]{0:T(128)} %bitcast.at_ref, bf16[512,512]{1,0:T(8,128)(2,1)S(1)} %bitcast.26, bf16[8,256,64]{2,1,0:T(8,128)(2,1)S(1)} %copy-done.2, f32[128,512]{1,0:T(8,128)S(1)} %copy-done, f32[128,512]{1,0:T(8,128)S(1)} %copy-done.1, bf16[128,1024]{1,0:T(8,128)(2,1)S(1)} %pad_maximum_fusion.1.e_ref, ...), custom_call_target="tpu_custom_call" | custom-call | tf_op jit(solution)/shard_map/forward_share/pallas_call | solution.py:221
  37.1 9.2 %all_to_all.15.part_ref = bf16[8,8,2,512]{3,2,1,0:T(2,128)(2,1)S(1)} all-to-all(bf16[8,8,2,512]{3,2,1,0:T(2,128)(2,1)S(1)} %forward_share.1), channel_id=1, replica_groups=mesh['facet'=8,'sub'=16] {'facet'}, dimensions={0} | all-to-all | bytes 262144 | tf_op jit(solution)/shard_map/all_to_all | solution.py:237
  46.3 5.9 %backward_share.1 = (f32[2,512]{1,0:T(2,128)S(1)}, bf16[512,512]{1,0:T(8,128)(2,1)}) custom-call(s32[1]{0:T(128)} %bitcast.at_ref, bf16[8,8,2,512]{3,2,1,0:T(2,128)(2,1)S(1)} %all_to_all.15.part_ref, bf16[128,1024]{1,0:T(8,128)(2,1)S(1)} %pad_maximum_fusion.1.e_ref, f32[128,512]{1,0:T(8,128)S(1)} %copy-done, f32[128,512]{1,0:T(8,128)S(1)} %copy-done.1, ...), custom_call_target="tpu_custom_call" | custom-call | tf_op jit(solution)/shard_map/backward_share/pallas_call | solution.py:239
  52.2 3.6 %all-to-all-start.2 = ((bf16[16,2,16,512]{3,2,1,0:T(8,128)(2,1)}), bf16[16,2,16,512]{3,2,1,0:T(8,128)(2,1)S(1)}, u32[]{:S(2)}, u32[]{:S(2)}) async-start(bf16[16,2,16,512]{3,2,1,0:T(8,128)(2,1)} %bitcast.9), calls=%async_computation.2 | async-start | bytes 1048576 | tf_op jit(solution)/shard_map/all_to_all | solution.py:257
  55.8 0.6 copy.13
  56.4 9.9 %all-to-all-done.2 = bf16[16,2,16,512]{3,2,1,0:T(8,128)(2,1)S(1)} async-done(((bf16[16,2,16,512]{3,2,1,0:T(8,128)(2,1)}), bf16[16,2,16,512]{3,2,1,0:T(8,128)(2,1)S(1)}, u32[]{:S(2)}, u32[]{:S(2)}) %all-to-all-start.2) | async-done | bytes 524320 | tf_op jit(solution)/shard_map/all_to_all | solution.py:257
  66.3 0.7 %convert_reduce_fusion = f32[2,16,512]{2,1,0:T(8,128)} fusion(bf16[16,2,16,512]{3,2,1,0:T(8,128)(2,1)S(1)} %all-to-all-done.2), kind=kLoop, calls=%fused_computation | loop fusion | flops 507904 | bytes 589824 | tf_op jit(solution)/shard_map/reduce_sum | solution.py:258
  (42 shorter events, 0.4 us)
Async XLA Ops:
  1.3 0.7 %copy-start.6 = (s32[1,512]{1,0:T(1,128)S(1)}, s32[1,512]{1,0:T(1,128)}, u32[]{:S(2)}) copy-start(s32[1,512]{1,0:T(1,128)} %param.13) | copy-start | bytes 6148
  1.3 0.7 %copy-start.7 = (s32[1,512]{1,0:T(1,128)S(1)}, s32[1,512]{1,0:T(1,128)}, u32[]{:S(2)}) copy-start(s32[1,512]{1,0:T(1,128)} %param.14) | copy-start | bytes 6148
  2.0 0.7 %copy-start.5 = (f32[2,1,512]{2,1,0:T(1,128)S(1)}, f32[2,1,512]{2,1,0:T(1,128)}, u32[]{:S(2)}) copy-start(f32[2,1,512]{2,1,0:T(1,128)} %param.15) | copy-start | bytes 12292
  2.0 11.8 %copy-start.4 = (bf16[2,16,512]{2,1,0:T(8,128)(2,1)S(1)}, bf16[2,16,512]{2,1,0:T(8,128)(2,1)}, u32[]{:S(2)}) copy-start(bf16[2,16,512]{2,1,0:T(8,128)(2,1)} %param.10) | copy-start | bytes 98308
  3.4 7.9 %collective-permute-start = (f32[8,512]{1,0:T(8,128)S(1)}, f32[8,512]{1,0:T(8,128)S(1)}, u32[]{:S(2)}, u32[]{:S(2)}) collective-permute-start(f32[8,512]{1,0:T(8,128)S(1)} %concatenate.19.refs_0_), channel_id=1, source_target_pairs={{0,16},{16,32},{32,48},{48,64},{64,80},{80,96},{96,112},{112,0},{1... | collective-permute-start | bytes 49160 | tf_op jit(solution)/shard_map/ppermute | solution.py:196
  6.1 6.1 %collective-permute-start.1 = (f32[8,512]{1,0:T(8,128)S(1)}, f32[8,512]{1,0:T(8,128)S(1)}, u32[]{:S(2)}, u32[]{:S(2)}) collective-permute-start(f32[8,512]{1,0:T(8,128)S(1)} %concatenate.19.refs_0_), channel_id=1, source_target_pairs={{0,32},{16,48},{32,64},{48,80},{64,96},{80,112},{96,0},{112,16},{1... | collective-permute-start | bytes 49160 | tf_op jit(solution)/shard_map/ppermute | solution.py:196
  7.4 15.0 %collective-permute-start.2 = (f32[8,512]{1,0:T(8,128)S(1)}, f32[8,512]{1,0:T(8,128)S(1)}, u32[]{:S(2)}, u32[]{:S(2)}) collective-permute-start(f32[8,512]{1,0:T(8,128)S(1)} %concatenate.19.refs_0_), channel_id=1, source_target_pairs={{0,48},{16,64},{32,80},{48,96},{64,112},{80,0},{96,16},{112,32},{1... | collective-permute-start | bytes 49160 | tf_op jit(solution)/shard_map/ppermute | solution.py:196
  9.1 13.3 %collective-permute-start.3 = (f32[8,512]{1,0:T(8,128)S(1)}, f32[8,512]{1,0:T(8,128)S(1)}, u32[]{:S(2)}, u32[]{:S(2)}) collective-permute-start(f32[8,512]{1,0:T(8,128)S(1)} %concatenate.19.refs_0_), channel_id=1, source_target_pairs={{0,64},{16,80},{32,96},{48,112},{64,0},{80,16},{96,32},{112,48},{1... | collective-permute-start | bytes 49160 | tf_op jit(solution)/shard_map/ppermute | solution.py:196
  9.4 13.0 %collective-permute-start.4 = (f32[8,512]{1,0:T(8,128)S(1)}, f32[8,512]{1,0:T(8,128)S(1)}, u32[]{:S(2)}, u32[]{:S(2)}) collective-permute-start(f32[8,512]{1,0:T(8,128)S(1)} %concatenate.19.refs_0_), channel_id=1, source_target_pairs={{0,80},{16,96},{32,112},{48,0},{64,16},{80,32},{96,48},{112,64},{1... | collective-permute-start | bytes 49160 | tf_op jit(solution)/shard_map/ppermute | solution.py:196
  11.3 11.1 %collective-permute-start.5 = (f32[8,512]{1,0:T(8,128)S(1)}, f32[8,512]{1,0:T(8,128)S(1)}, u32[]{:S(2)}, u32[]{:S(2)}) collective-permute-start(f32[8,512]{1,0:T(8,128)S(1)} %concatenate.19.refs_0_), channel_id=1, source_target_pairs={{0,96},{16,112},{32,0},{48,16},{64,32},{80,48},{96,64},{112,80},{1... | collective-permute-start | bytes 49160 | tf_op jit(solution)/shard_map/ppermute | solution.py:196
  12.2 10.3 %collective-permute-start.6 = (f32[8,512]{1,0:T(8,128)S(1)}, f32[8,512]{1,0:T(8,128)S(1)}, u32[]{:S(2)}, u32[]{:S(2)}) collective-permute-start(f32[8,512]{1,0:T(8,128)S(1)} %concatenate.19.refs_0_), channel_id=1, source_target_pairs={{0,112},{16,0},{32,16},{48,32},{64,48},{80,64},{96,80},{112,96},{1... | collective-permute-start | bytes 49160 | tf_op jit(solution)/shard_map/ppermute | solution.py:196
  14.7 18.7 %all-to-all-start = ((bf16[16,2,16,512]{3,2,1,0:T(8,128)(2,1)}), bf16[16,2,16,512]{3,2,1,0:T(8,128)(2,1)S(1)}, u32[]{:S(2)}, u32[]{:S(2)}) async-start(bf16[16,2,16,512]{3,2,1,0:T(8,128)(2,1)} %broadcast_in_dim.17), calls=%async_computation | async-start | bytes 1048576 | tf_op jit(solution)/shard_map/all_to_all | solution.py:30
  23.6 9.7 %copy-start.2 = (bf16[8,256,64]{2,1,0:T(8,128)(2,1)S(1)}, bf16[8,256,64]{2,1,0:T(8,128)(2,1)}, u32[]{:S(2)}) copy-start(bf16[8,256,64]{2,1,0:T(8,128)(2,1)} %constant.58.clone.d_ref) | copy-start | bytes 786436
  23.7 9.7 %copy-start = (f32[128,512]{1,0:T(8,128)S(1)}, f32[128,512]{1,0:T(8,128)}, u32[]{:S(2)}) copy-start(f32[128,512]{1,0:T(8,128)} %constant.60.clone.tc_ref) | copy-start | bytes 786436
  23.7 9.6 %copy-start.1 = (f32[128,512]{1,0:T(8,128)S(1)}, f32[128,512]{1,0:T(8,128)}, u32[]{:S(2)}) copy-start(f32[128,512]{1,0:T(8,128)} %constant.61.clone.ts_ref) | copy-start | bytes 786436
  37.0 9.2 %copy-start.3 = (bf16[8,32,256]{2,1,0:T(8,128)(2,1)S(1)}, bf16[8,32,256]{2,1,0:T(8,128)(2,1)}, u32[]{:S(2)}) copy-start(bf16[8,32,256]{2,1,0:T(8,128)(2,1)} %constant.59.clone.d_ref) | copy-start | bytes 393220
  52.2 14.1 %all-to-all-start.2 = ((bf16[16,2,16,512]{3,2,1,0:T(8,128)(2,1)}), bf16[16,2,16,512]{3,2,1,0:T(8,128)(2,1)S(1)}, u32[]{:S(2)}, u32[]{:S(2)}) async-start(bf16[16,2,16,512]{3,2,1,0:T(8,128)(2,1)} %bitcast.9), calls=%async_computation.2 | async-start | bytes 1048576 | tf_op jit(solution)/shard_map/all_to_all | solution.py:257
where the time goes:
time: 68 us; the launch traced here: 67 us
  starting transfers between devices  21.6 us (32%)
  waiting for transfers between devices  19.5 us (29%)
  Pallas kernels  9.66 us (14%)
  blocking collectives  9.19 us (14%)
  local copies, waits for them, and re-layouts  3.44 us (5%)
  between operations  2.23 us (3%)
  other arithmetic  1.39 us (2%)
    ppermute x7, starting transfers between devices, shards(): metas.append(lax.ppermute(meta, 'facet', ring))  10.4 us
    all_to_all x1, waiting for transfers between devices, shards(): image = lax.all_to_all(image, 'sub', 0, 0, tiled=True)  9.88 us
    all_to_all x1, waiting for transfers between devices, gather_by_exchange(): return lax.all_to_all(copies, axis, 0, 0, tiled=True)  9.6 us
    all_to_all x1, blocking collectives, shards(): parts = lax.all_to_all(part, 'facet', 0, 0, tiled=True)  9.19 us
    all_to_all x1, starting transfers between devices, gather_by_exchange(): return lax.all_to_all(copies, axis, 0, 0, tiled=True)  7.6 us
    pallas_call x1, Pallas kernels, shards(): pl.pallas_call(backward_kernel, out_shape=(jax.ShapeDtypeStruct((2, slots...  5.94 us
    pallas_call x1, Pallas kernels, shards(): pl.pallas_call(forward_kernel, out_shape=jax.ShapeDtypeStruct((facets, fa...  3.71 us
    all_to_all x1, starting transfers between devices, shards(): image = lax.all_to_all(image, 'sub', 0, 0, tiled=True)  3.57 us
  transfers between devices with their start and end apart: 9, of which 2 were waited for; matrix products, arithmetic and copies ran while one was open for 4% of the time, Pallas kernels for 0%

commit v1 on v0

v1 whole, which is shorter than its diff:
```python
import math

import jax
import jax.numpy as jnp
import numpy as np
from jax import lax
from jax.experimental import pallas as pl
from jax.experimental.pallas import tpu as pltpu
from jax.sharding import PartitionSpec as P

SG = 512
KS = 8
OVER = 16
RES = 128
KB = SG // RES
BATCH = 2
CHUNK = 16
WAVE = 8
SUB = 8
ROWS = 8
BF = jnp.bfloat16
F32 = jnp.float32


def split(value):
    high = lax.reduce_precision(value, 8, 7)
    return high.astype(BF), (value - high).astype(BF)


def gather_by_exchange(value, axis):
    count = lax.axis_size(axis)
    copies = jnp.broadcast_to(value[None], (count,) + value.shape)
    return lax.all_to_all(copies, axis, 0, 0, tiled=True)


def block_tables(facets, subs):
    block = np.arange(facets * subs).reshape(facets, subs)
    turn = (np.arange(RES)[None, :, None] * block[:, None, :]) % RES
    angle = turn * (2.0 * math.pi / RES)
    cos, sin = np.cos(angle), np.sin(angle)
    top = np.stack([cos, sin], -1)
    low = np.stack([-sin, cos], -1)
    table = np.concatenate([top, low], 1).reshape(facets, 2 * RES, 2 * subs)
    return table.astype(np.float32)


def host_split(table):
    high = table.astype(jnp.bfloat16)
    return high, (table - high.astype(np.float32)).astype(jnp.bfloat16)


def weights(fine_index, cells):
    middle = fine_index / OVER + (KS - 1) / 2.0
    cell = jnp.floor(fine_index / OVER)
    row = lax.broadcasted_iota(jnp.int32, (cells, fine_index.shape[1]), 0).astype(F32)
    distance = (row - middle) / 0.6
    weight = jnp.exp(-0.5 * (distance * distance))
    return jnp.where((row >= cell) & (row < cell + KS), weight, F32(0.0))


def weight_rows(fine_index, cells):
    cell = jnp.floor(fine_index / OVER)
    tile = jnp.floor(cell / KS)
    inner = cell - tile * KS
    row = lax.broadcasted_iota(jnp.int32, (KS, fine_index.shape[1]), 0).astype(F32)
    wrapped = row < inner
    offset = row - inner + jnp.where(wrapped, F32(KS), F32(0.0))
    distance = (offset - ((KS - 1) / 2.0 + (fine_index / OVER - cell))) / 0.6
    weight = jnp.exp(-0.5 * (distance * distance))
    tile = tile + jnp.where(wrapped, F32(1.0), F32(0.0))
    return [jnp.where(tile == F32(n), weight, F32(0.0)) for n in range(cells // KS)]


def dot(left, right, dims):
    return lax.dot_general(left, right, (dims, ((), ())), preferred_element_type=F32)


def slot_rows(refs, slot):
    start = (slot % 2) * ROWS
    return refs[slot // 2], start


def slot_place(at, slot, groups):
    return ((at - (slot // 2) * 2) & (groups - 1)) ^ (slot % 2)


def pack_kernel(pos_ref, cnt_ref, u_ref, v_ref, obs_ref, *refs):
    meta_ref = refs[-1]
    slots = u_ref.shape[1]
    meta_ref[0:1, :] = u_ref[...].astype(F32)
    meta_ref[1:2, :] = v_ref[...].astype(F32)
    meta_ref[2:3, :] = obs_ref[0]
    meta_ref[3:4, :] = obs_ref[1]
    meta_ref[4:5, :] = jnp.full((1, slots), pos_ref[0] // RES, jnp.int32).astype(F32)
    meta_ref[5:6, :] = jnp.full((1, slots), cnt_ref[0], jnp.int32).astype(F32)
    meta_ref[6:8, :] = jnp.zeros((2, slots), F32)


def expand(wu_ref, fine_index):
    rows = weight_rows(fine_index, wu_ref.shape[0])
    for n in range(0, len(rows), 2):
        wu_ref[n * KS : (n + 2) * KS, :] = jnp.concatenate(rows[n : n + 2], 0).astype(BF)


def forward_kernel(at_ref, y_ref, d_ref, tc_ref, ts_ref, e_ref, *refs):
    meta_refs = refs[:-4]
    part_ref, ys_ref, gs_ref, wu_ref = refs[-4:]
    groups = 2 * len(meta_refs)
    d_table = d_ref[at_ref[0]]
    pieces = y_ref.shape[0]
    half = e_ref.shape[0] // 2
    band = half // KB
    rows_v = gs_ref.shape[1] // band
    lines = pieces // rows_v
    for k in range(KB):
        ys_ref[k] = y_ref[:, k * RES : (k + 1) * RES].astype(F32)
    for v in range(0, rows_v, BATCH):
        turned = []
        for n in range(BATCH):
            row = [ys_ref[k, pl.ds(v + n, lines, stride=rows_v), :] for k in range(KB)]
            row = jnp.concatenate(row, 1).astype(BF)
            spread = dot(d_table, jnp.concatenate([row, row], 0), ((1,), (0,)))
            spread = spread.reshape(RES // SUB, 2, SUB, SG)
            real_g, imag_g = spread[:, 0], spread[:, 1]
            cos = tc_ref[...].reshape(RES // SUB, SUB, SG)
            sin = ts_ref[...].reshape(RES // SUB, SUB, SG)
            real_h = (real_g * cos + imag_g * sin).reshape(RES, SG).astype(BF)
            imag_h = (imag_g * cos - real_g * sin).reshape(RES, SG).astype(BF)
            turned.append(jnp.concatenate([real_h, imag_h], 1))
        share = dot(e_ref[...], jnp.concatenate(turned, 0), ((1,), (1,)))
        share = share[:half] + share[half:]
        for n in range(BATCH):
            for k in range(KB):
                gs_ref[k, pl.ds(v + n, band, stride=rows_v), :] = share[
                    k * band : (k + 1) * band, n * RES : (n + 1) * RES
                ]
    for s in range(groups):
        grid = [gs_ref[k, s * 2 * rows_v : (s + 1) * 2 * rows_v, :] for k in range(KB)]
        grid = jnp.concatenate(grid, 1)
        high = grid.astype(BF)
        low = (grid - high.astype(F32)).astype(BF)
        meta, start = slot_rows(meta_refs, s)
        expand(wu_ref.at[s], meta[start : start + 1, :])
        along = dot(jnp.concatenate([high, low], 0), wu_ref[s], ((1,), (0,)))
        along = along[: 2 * rows_v] + along[2 * rows_v :]
        wv = weights(meta[start + 1 : start + 2, :], rows_v)
        real = jnp.sum(along[:rows_v] * wv, 0, keepdims=True)
        imag = jnp.sum(along[rows_v:] * wv, 0, keepdims=True)
        place = slot_place(at_ref[0], s, groups)
        both = jnp.concatenate([real, imag], 0).astype(BF)
        for n in range(groups):
            part_ref[n, place] = both


def backward_kernel(at_ref, part_ref, e_ref, tc_ref, ts_ref, d_ref, *refs):
    meta_refs = refs[:-8]
    res_ref, out_ref, pred_ref, rs_ref, im_ref, wu_ref, ct_ref, m_ref = refs[-8:]
    groups = 2 * len(meta_refs)
    slots = res_ref.shape[2]
    d_table = d_ref[at_ref[0]]
    lines = d_table.shape[0]
    band = 2 * groups
    rows_v = rs_ref.shape[1] // band
    pred_ref[...] = jnp.sum(part_ref[...].astype(F32), 0)
    slot = lax.broadcasted_iota(jnp.int32, (2, slots), 1).astype(F32)
    for s in range(groups):
        place = slot_place(at_ref[0], s, groups)
        meta, start = slot_rows(meta_refs, s)
        seen = meta[start + 2 : start + 4, :] - pred_ref[place]
        residual = jnp.where(slot < meta[start + 5 : start + 6, :], seen, F32(0.0))
        if s == 0:
            res_ref[0] = residual[0:1]
            res_ref[1] = residual[1:2]
        wv = weights(meta[start + 1 : start + 2, :], rows_v)
        spread = jnp.concatenate([wv * residual[0:1], wv * residual[1:2]], 0).astype(BF)
        expand(wu_ref.at[s], meta[start : start + 1, :])
        cells = dot(spread, wu_ref[s], ((1,), (1,)))
        for k in range(KB):
            rs_ref[k, s * 2 * rows_v : (s + 1) * 2 * rows_v, :] = cells[:, k * RES : (k + 1) * RES]
    for v in range(rows_v):
        rows = [rs_ref[k, pl.ds(v, band, stride=rows_v), :] for k in range(KB)]
        ct_ref[v] = jnp.concatenate(rows, 0).T.astype(BF)
    e_table = e_ref[: KB * band, :]
    for f in range(0, RES, CHUNK):
        cos = tc_ref[f : f + CHUNK, :]
        sin = ts_ref[f : f + CHUNK, :]
        for v in range(0, rows_v, WAVE):
            cells = ct_ref[v : v + WAVE, f : f + CHUNK, :].reshape(WAVE * CHUNK, KB * band)
            back = dot(cells, e_table, ((1,), (0,))).reshape(WAVE, CHUNK, 2 * SG)
            real_b, imag_b = back[..., :SG], back[..., SG:]
            m_ref[v : v + WAVE, f : f + CHUNK, :] = (real_b * cos - imag_b * sin).astype(BF)
            m_ref[v : v + WAVE, RES + f : RES + f + CHUNK, :] = (
                imag_b * cos + real_b * sin
            ).astype(BF)
    for v in range(rows_v):
        image = dot(d_table, m_ref[v], ((1,), (0,)))
        for k in range(KB):
            im_ref[k, pl.ds(v, lines, stride=rows_v), :] = image[:, k * RES : (k + 1) * RES]
    for k in range(KB):
        out_ref[:, k * RES : (k + 1) * RES] = im_ref[k].astype(BF)


def shards(facet_data, subgrid_pos, vis_counts, vis_u_fine, vis_v_fine, vis_observed):
    facets = lax.axis_size("facet")
    subs = lax.axis_size("sub")
    rows_v = facet_data.shape[1]
    slots = vis_u_fine.shape[1]
    facet = lax.axis_index("facet")
    inside = jnp.arange(SG, dtype=jnp.int32)

    gathered = gather_by_exchange(facet_data, "sub")

    table = block_tables(facets, subs)
    high_d, low_d = host_split(table)
    into = np.concatenate([high_d, low_d], 2)
    into = into.reshape(facets, 2, RES // SUB, SUB, -1).swapaxes(1, 2)
    into = jnp.asarray(into.reshape(facets, 2 * RES, -1))
    outof = jnp.asarray(high_d.transpose(0, 2, 1))
    turn = np.arange(RES)[:, None] * np.arange(SG)[None, :] * (2.0 * math.pi / 65536)
    tw_cos = jnp.asarray(np.cos(turn).astype(np.float32))
    tw_sin = jnp.asarray(np.sin(turn).astype(np.float32))
    params = pltpu.CompilerParams(vmem_limit_bytes=24 * 1024 * 1024)
    vmem = pl.BlockSpec(memory_space=pltpu.VMEM)
    smem = pl.BlockSpec(memory_space=pltpu.SMEM)
    meta = pl.pallas_call(
        pack_kernel,
        out_shape=jax.ShapeDtypeStruct((ROWS, slots), F32),
        in_specs=[smem] * 2 + [vmem] * 7,
        out_specs=vmem,
        compiler_params=params,
        name="pack_meta",
    )(
        subgrid_pos, vis_counts, vis_u_fine, vis_v_fine, vis_observed,
        into, outof, tw_cos, tw_sin,
    )
    partner = lax.ppermute(meta, "facet", [(n, n ^ 1) for n in range(facets)])
    pairs = [jnp.concatenate([meta, partner], 0)]
    for d in range(2, facets, 2):
        ring = [(n, (n + d) % facets) for n in range(facets)]
        pairs.append(lax.ppermute(pairs[0], "facet", ring))

    spot = jnp.concatenate([p[n : n + 1] for p in pairs for n in (4, 4 + ROWS)], 0)
    spot = spot.astype(jnp.int32)
    step = spot[None] + jnp.arange(KB, dtype=jnp.int32)[:, None, None]
    turn = (step * inside).reshape(KB * facets, SG) % SG
    angle = turn.astype(F32) * (2.0 * math.pi / SG)
    scale = F32(1.0 / 256.0)
    cos, sin = jnp.cos(angle) * scale, jnp.sin(angle) * scale
    lines = jnp.stack(
        [jnp.concatenate([cos, sin], 1), jnp.concatenate([-sin, cos], 1)], 1
    ).reshape(2 * KB * facets, 2 * SG)
    high_e, low_e = split(lines)
    e_table = jnp.concatenate([high_e, low_e], 0)

    at = facet.astype(jnp.int32)[None]
    part = pl.pallas_call(
        forward_kernel,
        out_shape=jax.ShapeDtypeStruct((facets, facets, 2, slots), BF),
        in_specs=[smem] + [vmem] * (5 + facets // 2),
        scratch_shapes=[
            pltpu.VMEM((KB, 2 * subs * rows_v, RES), F32),
            pltpu.VMEM((KB, 2 * facets * rows_v, RES), F32),
            pltpu.VMEM((facets, SG, slots), BF),
        ],
        compiler_params=params,
        name="forward_share",
    )(
        at, gathered.reshape(2 * subs * rows_v, SG), into, tw_cos, tw_sin, e_table,
        *pairs,
    )

    parts = lax.all_to_all(part, "facet", 0, 0, tiled=True)

    residual, image = pl.pallas_call(
        backward_kernel,
        out_shape=(
            jax.ShapeDtypeStruct((2, 1, slots), F32),
            jax.ShapeDtypeStruct((2 * subs * rows_v, SG), BF),
        ),
        in_specs=[smem] + [vmem] * (5 + facets // 2),
        scratch_shapes=[
            pltpu.VMEM((facets, 2, slots), F32),
            pltpu.VMEM((KB, 2 * facets * rows_v, RES), F32),
            pltpu.VMEM((KB, 2 * subs * rows_v, RES), F32),
            pltpu.VMEM((facets, SG, slots), BF),
            pltpu.VMEM((rows_v, RES, 2 * KB * facets), BF),
            pltpu.VMEM((rows_v, 2 * RES, SG), BF),
        ],
        compiler_params=params,
        name="backward_share",
    )(at, parts, e_table, tw_cos, tw_sin, outof, *pairs)

    image = image.reshape(subs, 2, rows_v, SG)
    image = lax.all_to_all(image, "sub", 0, 0, tiled=True)
    return (residual, jnp.sum(image.astype(F32), 0))


def solution(mesh):
    return jax.shard_map(
        shards,
        mesh=mesh,
        in_specs=(
            P(None, None, ("facet", "sub")),
            P(("facet", "sub")),
            P(("facet", "sub")),
            P(("facet", "sub"), None),
            P(("facet", "sub"), None),
            P(None, ("facet", "sub"), None),
        ),
        out_specs=(P(None, ("facet", "sub"), None), P(None, None, ("facet", "sub"))),
        check_vma=False,
    )
```

time: 68 us -> 65.8 us (0.968)
  blocking collectives: 9.19 us -> 25.9 us
  waiting for transfers between devices: 19.5 us -> 6.25 us
  starting transfers between devices: 21.6 us -> 14.2 us
  local copies, waits for them, and re-layouts: 3.44 us -> 6.67 us
  Pallas kernels: 9.66 us -> 8.18 us
    all_to_all x0 -> x1, blocking collectives: none -> 14.6 us  [shards(): image = lax.all_to_all(image, 'sub', 0, 0, tiled=True)]
    all_to_all x1 -> x0, waiting for transfers between devices: 9.88 us -> none  [shards(): image = lax.all_to_all(image, 'sub', 0, 0, tiled=True)]
    all_to_all x1, waiting for transfers between devices: 9.6 us -> 3.44 us  [gather_by_exchange(): return lax.all_to_all(copies, axis, 0, 0, tiled=True)]
    ppermute x7 -> x4, starting transfers between devices: 10.4 us -> 6.57 us  [the longest x3 5.11 us: shards(): pairs.append(lax.ppermute(pairs[0], 'facet', ring))]
    all_to_all x1 -> x0, starting transfers between devices: 3.57 us -> none  [shards(): image = lax.all_to_all(image, 'sub', 0, 0, tiled=True)]
    unnamed x17 -> x24, local copies, waits for them, and re-layouts: 1.96 us -> 5.24 us
    ppermute x7 -> x4, waiting for transfers between devices: 0.02 us -> 2.81 us  [the longest x3 1.97 us: shards(): pairs.append(lax.ppermute(pairs[0], 'facet', ring))]
    all_to_all x1, blocking collectives: 9.19 us -> 11.4 us  [shards(): parts = lax.all_to_all(part, 'facet', 0, 0, tiled=True)]
  transfers between devices with their start and end apart: 9 -> 5, of which waited for: 2 -> 4; matrix products, arithmetic and copies ran while one was open for 4% -> 3% of each run, Pallas kernels for 0% -> 0%
where the time goes in v1:
time: 65.8 us; the launch traced here: 64.7 us
  blocking collectives  25.9 us (39%)
  starting transfers between devices  14.2 us (22%)
  Pallas kernels  8.18 us (12%)
  local copies, waits for them, and re-layouts  6.67 us (10%)
  waiting for transfers between devices  6.25 us (9%)
  between operations  2.12 us (3%)
  other arithmetic  1.38 us (2%)
    all_to_all x1, blocking collectives, shards(): image = lax.all_to_all(image, 'sub', 0, 0, tiled=True)  14.6 us
    all_to_all x1, blocking collectives, shards(): parts = lax.all_to_all(part, 'facet', 0, 0, tiled=True)  11.4 us
    all_to_all x1, starting transfers between devices, gather_by_exchange(): return lax.all_to_all(copies, axis, 0, 0, tiled=True)  7.6 us
    unnamed x24, local copies, waits for them, and re-layouts  5.24 us
    ppermute x3, starting transfers between devices, shards(): pairs.append(lax.ppermute(pairs[0], 'facet', ring))  5.11 us
    pallas_call x1, Pallas kernels, shards(): pl.pallas_call(backward_kernel, out_shape=(jax.ShapeDtypeStruct((2, 1, sl...  4.41 us
    pallas_call x1, Pallas kernels, shards(): pl.pallas_call(forward_kernel, out_shape=jax.ShapeDtypeStruct((facets, fa...  3.76 us
    all_to_all x1, waiting for transfers between devices, gather_by_exchange(): return lax.all_to_all(copies, axis, 0, 0, tiled=True)  3.44 us
  transfers between devices with their start and end apart: 5, of which 4 were waited for; matrix products, arithmetic and copies ran while one was open for 3% of the time, Pallas kernels for 0%

profile of v1, /device:TPU:1, one launch (start us, length us, event | category | flops | bytes accessed | tf_op | source)
XLA Modules:
  0.0 64.7 jit_solution(14034028422736121150)
XLA Ops:
  2.0 0.9 %copy-done = f32[128,512]{1,0:T(8,128)S(1)} copy-done((f32[128,512]{1,0:T(8,128)S(1)}, f32[128,512]{1,0:T(8,128)}, u32[]{:S(2)}) %copy-start) | copy-done | bytes 262168
  2.9 0.9 %copy-done.2 = f32[128,512]{1,0:T(8,128)S(1)} copy-done((f32[128,512]{1,0:T(8,128)S(1)}, f32[128,512]{1,0:T(8,128)}, u32[]{:S(2)}) %copy-start.2) | copy-done | bytes 262168
  3.9 1.0 %copy-done.4 = bf16[8,256,64]{2,1,0:T(8,128)(2,1)S(1)} copy-done((bf16[8,256,64]{2,1,0:T(8,128)(2,1)S(1)}, bf16[8,256,64]{2,1,0:T(8,128)(2,1)}, u32[]{:S(2)}) %copy-start.4) | copy-done | bytes 262168
  4.9 0.9 %copy-done.6 = bf16[8,32,256]{2,1,0:T(8,128)(2,1)S(1)} copy-done((bf16[8,32,256]{2,1,0:T(8,128)(2,1)S(1)}, bf16[8,32,256]{2,1,0:T(8,128)(2,1)}, u32[]{:S(2)}) %copy-start.6) | copy-done | bytes 131096
  5.8 0.7 %copy-done.8 = f32[2,1,512]{2,1,0:T(1,128)S(1)} copy-done((f32[2,1,512]{2,1,0:T(1,128)S(1)}, f32[2,1,512]{2,1,0:T(1,128)}, u32[]{:S(2)}) %copy-start.8) | copy-done | bytes 4120
  6.5 0.7 %copy-done.10 = s32[1,512]{1,0:T(1,128)S(1)} copy-done((s32[1,512]{1,0:T(1,128)S(1)}, s32[1,512]{1,0:T(1,128)}, u32[]{:S(2)}) %copy-start.10) | copy-done | bytes 2072
  7.2 1.5 %collective-permute-start = (f32[8,512]{1,0:T(8,128)S(1)}, f32[8,512]{1,0:T(8,128)S(1)}, u32[]{:S(2)}, u32[]{:S(2)}) collective-permute-start(f32[8,512]{1,0:T(8,128)S(1)} %pack_meta.1), channel_id=1, source_target_pairs={{0,16},{16,0},{32,48},{48,32},{64,80},{80,64},{96,112},{112,96},{1... | collective-permute-start | bytes 49160 | tf_op jit(solution)/shard_map/ppermute | solution.py:236
  8.6 0.8 %collective-permute-done = f32[8,512]{1,0:T(8,128)S(1)} collective-permute-done((f32[8,512]{1,0:T(8,128)S(1)}, f32[8,512]{1,0:T(8,128)S(1)}, u32[]{:S(2)}, u32[]{:S(2)}) %collective-permute-start) | collective-permute-done | bytes 16416 | tf_op jit(solution)/shard_map/ppermute | solution.py:236
  9.5 1.4 %collective-permute-start.1 = (f32[16,512]{1,0:T(8,128)S(1)}, f32[16,512]{1,0:T(8,128)S(1)}, u32[]{:S(2)}, u32[]{:S(2)}) collective-permute-start(f32[16,512]{1,0:T(8,128)S(1)} %pad_maximum_fusion.3.refs_0_), channel_id=1, source_target_pairs={{0,32},{16,48},{32,64},{48,80},{64,96},{80,112},{96,0},{112,16},{1... | collective-permute-start | bytes 98312 | tf_op jit(solution)/shard_map/ppermute | solution.py:240
  10.9 0.9 %broadcast_in_dim.5 = bf16[16,2,16,512]{3,2,1,0:T(8,128)(2,1)} broadcast(bf16[2,16,512]{2,1,0:T(8,128)(2,1)S(1)} %copy-done.11), dimensions={1,2,3} | broadcast | bytes 557056 | tf_op jit(solution)/shard_map/broadcast_in_dim | solution.py:32
  11.8 7.6 %all-to-all-start = ((bf16[16,2,16,512]{3,2,1,0:T(8,128)(2,1)}), bf16[16,2,16,512]{3,2,1,0:T(8,128)(2,1)S(1)}, u32[]{:S(2)}, u32[]{:S(2)}) async-start(bf16[16,2,16,512]{3,2,1,0:T(8,128)(2,1)} %broadcast_in_dim.5), calls=%async_computation | async-start | bytes 1048576 | tf_op jit(solution)/shard_map/all_to_all | solution.py:33
  19.5 2.6 %collective-permute-start.2 = (f32[16,512]{1,0:T(8,128)S(1)}, f32[16,512]{1,0:T(8,128)S(1)}, u32[]{:S(2)}, u32[]{:S(2)}) collective-permute-start(f32[16,512]{1,0:T(8,128)S(1)} %pad_maximum_fusion.3.refs_0_), channel_id=1, source_target_pairs={{0,64},{16,80},{32,96},{48,112},{64,0},{80,16},{96,32},{112,48},{1... | collective-permute-start | bytes 98312 | tf_op jit(solution)/shard_map/ppermute | solution.py:240
  22.1 1.1 %collective-permute-start.3 = (f32[16,512]{1,0:T(8,128)S(1)}, f32[16,512]{1,0:T(8,128)S(1)}, u32[]{:S(2)}, u32[]{:S(2)}) collective-permute-start(f32[16,512]{1,0:T(8,128)S(1)} %pad_maximum_fusion.3.refs_0_), channel_id=1, source_target_pairs={{0,96},{16,112},{32,0},{48,16},{64,32},{80,48},{96,64},{112,80},{1... | collective-permute-start | bytes 98312 | tf_op jit(solution)/shard_map/ppermute | solution.py:240
  23.2 0.6 collective-permute-done.2.refs_2_
  23.8 1.4 %collective-permute-done.3.refs_3_ = f32[16,512]{1,0:T(8,128)S(1)} collective-permute-done((f32[16,512]{1,0:T(8,128)S(1)}, f32[16,512]{1,0:T(8,128)S(1)}, u32[]{:S(2)}, u32[]{:S(2)}) %collective-permute-start.3) | collective-permute-done | bytes 32800 | tf_op jit(solution)/shard_map/ppermute | solution.py:240
  25.2 0.4 sine_multiply_fusion
  25.9 0.2 pad_maximum_fusion
  26.1 0.2 reshape.75
  26.4 3.4 %all-to-all-done = bf16[16,2,16,512]{3,2,1,0:T(8,128)(2,1)S(1)} async-done(((bf16[16,2,16,512]{3,2,1,0:T(8,128)(2,1)}), bf16[16,2,16,512]{3,2,1,0:T(8,128)(2,1)S(1)}, u32[]{:S(2)}, u32[]{:S(2)}) %all-to-all-start) | async-done | bytes 524320 | tf_op jit(solution)/shard_map/all_to_all | solution.py:33
  29.9 3.8 %forward_share.1 = bf16[8,8,2,512]{3,2,1,0:T(2,128)(2,1)S(1)} custom-call(s32[1]{0:T(128)} %bitcast.at_ref, bf16[512,512]{1,0:T(8,128)(2,1)S(1)} %bitcast.19, bf16[8,256,64]{2,1,0:T(8,128)(2,1)S(1)} %copy-done.5, f32[128,512]{1,0:T(8,128)S(1)} %copy-done.1, f32[128,512]{1,0:T(8,128)S(1)} %copy-done.3, bf16[128,1024]{1,0:T(8,128)(2,1)S(1)} %pad_maximum_fusion.1.e_ref, ...), custom_call_target="tpu_custom_call" | custom-call | tf_op jit(solution)/shard_map/forward_share/pallas_call | solution.py:256
  33.6 11.4 %all_to_all.15.part_ref = bf16[8,8,2,512]{3,2,1,0:T(2,128)(2,1)S(1)} all-to-all(bf16[8,8,2,512]{3,2,1,0:T(2,128)(2,1)S(1)} %forward_share.1), channel_id=1, replica_groups=mesh['facet'=8,'sub'=16] {'facet'}, dimensions={0} | all-to-all | bytes 262144 | tf_op jit(solution)/shard_map/all_to_all | solution.py:272
  45.0 4.4 %backward_share.1 = (f32[2,1,512]{2,1,0:T(1,128)}, bf16[512,512]{1,0:T(8,128)(2,1)S(1)}) custom-call(s32[1]{0:T(128)} %bitcast.at_ref, bf16[8,8,2,512]{3,2,1,0:T(2,128)(2,1)S(1)} %all_to_all.15.part_ref, bf16[128,1024]{1,0:T(8,128)(2,1)S(1)} %pad_maximum_fusion.1.e_ref, f32[128,512]{1,0:T(8,128)S(1)} %copy-done.1, f32[128,512]{1,0:T(8,128)S(1)} %copy-done.3, ...), custom_call_target="tpu_custom_call" | custom-call | tf_op jit(solution)/shard_map/backward_share/pallas_call | solution.py:274
  49.4 14.6 %all_to_all.16 = bf16[16,2,16,512]{3,2,1,0:T(8,128)(2,1)S(1)} all-to-all(bf16[16,2,16,512]{3,2,1,0:T(8,128)(2,1)S(1)} %bitcast.20), channel_id=1, replica_groups=mesh['facet'=8,'sub'=16] {'sub'}, dimensions={0} | all-to-all | bytes 1048576 | tf_op jit(solution)/shard_map/all_to_all | solution.py:294
  64.0 0.7 %convert_reduce_fusion = f32[2,16,512]{2,1,0:T(8,128)} fusion(bf16[16,2,16,512]{3,2,1,0:T(8,128)(2,1)S(1)} %all_to_all.16), kind=kLoop, calls=%fused_computation | loop fusion | flops 507904 | bytes 589824 | tf_op jit(solution)/shard_map/reduce_sum | solution.py:295
  (35 shorter events, 0.5 us)
Async XLA Ops:
  0.6 1.3 %copy-start.9 = (s32[1,512]{1,0:T(1,128)S(1)}, s32[1,512]{1,0:T(1,128)}, u32[]{:S(2)}) copy-start(s32[1,512]{1,0:T(1,128)} %u_ref.1) | copy-start | bytes 6148
  2.0 1.0 %copy-start = (f32[128,512]{1,0:T(8,128)S(1)}, f32[128,512]{1,0:T(8,128)}, u32[]{:S(2)}) copy-start(f32[128,512]{1,0:T(8,128)} %constant.37.clone.refs_2_.tc_ref) | copy-start | bytes 786436
  2.9 0.9 %copy-start.2 = (f32[128,512]{1,0:T(8,128)S(1)}, f32[128,512]{1,0:T(8,128)}, u32[]{:S(2)}) copy-start(f32[128,512]{1,0:T(8,128)} %constant.38.clone.refs_3_.ts_ref) | copy-start | bytes 786436
  3.9 1.0 %copy-start.4 = (bf16[8,256,64]{2,1,0:T(8,128)(2,1)S(1)}, bf16[8,256,64]{2,1,0:T(8,128)(2,1)}, u32[]{:S(2)}) copy-start(bf16[8,256,64]{2,1,0:T(8,128)(2,1)} %constant.35.clone.refs_0_.d_ref) | copy-start | bytes 786436
  4.9 0.9 %copy-start.6 = (bf16[8,32,256]{2,1,0:T(8,128)(2,1)S(1)}, bf16[8,32,256]{2,1,0:T(8,128)(2,1)}, u32[]{:S(2)}) copy-start(bf16[8,32,256]{2,1,0:T(8,128)(2,1)} %constant.36.clone.refs_1_.d_ref) | copy-start | bytes 393220
  5.8 0.7 %copy-start.8 = (f32[2,1,512]{2,1,0:T(1,128)S(1)}, f32[2,1,512]{2,1,0:T(1,128)}, u32[]{:S(2)}) copy-start(f32[2,1,512]{2,1,0:T(1,128)} %obs_ref.1) | copy-start | bytes 12292
  6.5 0.7 %copy-start.10 = (s32[1,512]{1,0:T(1,128)S(1)}, s32[1,512]{1,0:T(1,128)}, u32[]{:S(2)}) copy-start(s32[1,512]{1,0:T(1,128)} %v_ref.1) | copy-start | bytes 6148
  7.2 3.7 %copy-start.11 = (bf16[2,16,512]{2,1,0:T(8,128)(2,1)S(1)}, bf16[2,16,512]{2,1,0:T(8,128)(2,1)}, u32[]{:S(2)}) copy-start(bf16[2,16,512]{2,1,0:T(8,128)(2,1)} %param.10) | copy-start | bytes 98308
  7.2 2.3 %collective-permute-start = (f32[8,512]{1,0:T(8,128)S(1)}, f32[8,512]{1,0:T(8,128)S(1)}, u32[]{:S(2)}, u32[]{:S(2)}) collective-permute-start(f32[8,512]{1,0:T(8,128)S(1)} %pack_meta.1), channel_id=1, source_target_pairs={{0,16},{16,0},{32,48},{48,32},{64,80},{80,64},{96,112},{112,96},{1... | collective-permute-start | bytes 49160 | tf_op jit(solution)/shard_map/ppermute | solution.py:236
  9.5 13.7 %collective-permute-start.1 = (f32[16,512]{1,0:T(8,128)S(1)}, f32[16,512]{1,0:T(8,128)S(1)}, u32[]{:S(2)}, u32[]{:S(2)}) collective-permute-start(f32[16,512]{1,0:T(8,128)S(1)} %pad_maximum_fusion.3.refs_0_), channel_id=1, source_target_pairs={{0,32},{16,48},{32,64},{48,80},{64,96},{80,112},{96,0},{112,16},{1... | collective-permute-start | bytes 98312 | tf_op jit(solution)/shard_map/ppermute | solution.py:240
  11.8 18.1 %all-to-all-start = ((bf16[16,2,16,512]{3,2,1,0:T(8,128)(2,1)}), bf16[16,2,16,512]{3,2,1,0:T(8,128)(2,1)S(1)}, u32[]{:S(2)}, u32[]{:S(2)}) async-start(bf16[16,2,16,512]{3,2,1,0:T(8,128)(2,1)} %broadcast_in_dim.5), calls=%async_computation | async-start | bytes 1048576 | tf_op jit(solution)/shard_map/all_to_all | solution.py:33
  19.5 4.3 %collective-permute-start.2 = (f32[16,512]{1,0:T(8,128)S(1)}, f32[16,512]{1,0:T(8,128)S(1)}, u32[]{:S(2)}, u32[]{:S(2)}) collective-permute-start(f32[16,512]{1,0:T(8,128)S(1)} %pad_maximum_fusion.3.refs_0_), channel_id=1, source_target_pairs={{0,64},{16,80},{32,96},{48,112},{64,0},{80,16},{96,32},{112,48},{1... | collective-permute-start | bytes 98312 | tf_op jit(solution)/shard_map/ppermute | solution.py:240
  22.1 3.1 %collective-permute-start.3 = (f32[16,512]{1,0:T(8,128)S(1)}, f32[16,512]{1,0:T(8,128)S(1)}, u32[]{:S(2)}, u32[]{:S(2)}) collective-permute-start(f32[16,512]{1,0:T(8,128)S(1)} %pad_maximum_fusion.3.refs_0_), channel_id=1, source_target_pairs={{0,96},{16,112},{32,0},{48,16},{64,32},{80,48},{96,64},{112,80},{1... | collective-permute-start | bytes 98312 | tf_op jit(solution)/shard_map/ppermute | solution.py:240
  26.3 3.6 %copy-start.5 = (bf16[8,256,64]{2,1,0:T(8,128)(2,1)S(1)}, bf16[8,256,64]{2,1,0:T(8,128)(2,1)}, u32[]{:S(2)}) copy-start(bf16[8,256,64]{2,1,0:T(8,128)(2,1)} %constant.35.clone.refs_0_.d_ref) | copy-start | bytes 786436
  26.4 3.5 %copy-start.1 = (f32[128,512]{1,0:T(8,128)S(1)}, f32[128,512]{1,0:T(8,128)}, u32[]{:S(2)}) copy-start(f32[128,512]{1,0:T(8,128)} %constant.37.clone.refs_2_.tc_ref) | copy-start | bytes 786436
  26.4 3.5 %copy-start.3 = (f32[128,512]{1,0:T(8,128)S(1)}, f32[128,512]{1,0:T(8,128)}, u32[]{:S(2)}) copy-start(f32[128,512]{1,0:T(8,128)} %constant.38.clone.refs_3_.ts_ref) | copy-start | bytes 786436
  33.6 11.4 %copy-start.7 = (bf16[8,32,256]{2,1,0:T(8,128)(2,1)S(1)}, bf16[8,32,256]{2,1,0:T(8,128)(2,1)}, u32[]{:S(2)}) copy-start(bf16[8,32,256]{2,1,0:T(8,128)(2,1)} %constant.36.clone.refs_1_.d_ref) | copy-start | bytes 393220

commit v2 on v1

--- a/solution.py
+++ b/solution.py
@@ -13,24 +13,13 @@
 OVER = 16
 RES = 128
 KB = SG // RES
-BATCH = 2
+BATCH = 4
 CHUNK = 16
-WAVE = 8
+WAVE = 4
 SUB = 8
 ROWS = 8
 BF = jnp.bfloat16
 F32 = jnp.float32
-
-
-def split(value):
-    high = lax.reduce_precision(value, 8, 7)
-    return high.astype(BF), (value - high).astype(BF)
-
-
-def gather_by_exchange(value, axis):
-    count = lax.axis_size(axis)
-    copies = jnp.broadcast_to(value[None], (count,) + value.shape)
-    return lax.all_to_all(copies, axis, 0, 0, tiled=True)
 
 
 def block_tables(facets, subs):
@@ -84,9 +73,28 @@
     return ((at - (slot // 2) * 2) & (groups - 1)) ^ (slot % 2)
 
 
-def pack_kernel(pos_ref, cnt_ref, u_ref, v_ref, obs_ref, *refs):
-    meta_ref = refs[-1]
+def lead_kernel(
+    pos_ref, cnt_ref, y_hbm, u_hbm, v_hbm, obs_hbm, copy_hbm, meta_ref,
+    y_ref, u_ref, v_ref, obs_ref, load_sem, send_sem,
+):
     slots = u_ref.shape[1]
+    loads = [
+        pltpu.make_async_copy(source, target, load_sem.at[n])
+        for n, (source, target) in enumerate(
+            [(y_hbm, y_ref), (u_hbm, u_ref), (v_hbm, v_ref), (obs_hbm, obs_ref)]
+        )
+    ]
+    for load in loads:
+        load.start()
+    loads[0].wait()
+    sends = [
+        pltpu.make_async_copy(y_ref, copy_hbm.at[n], send_sem.at[n])
+        for n in range(copy_hbm.shape[0])
+    ]
+    for send in sends:
+        send.start()
+    for load in loads[1:]:
+        load.wait()
     meta_ref[0:1, :] = u_ref[...].astype(F32)
     meta_ref[1:2, :] = v_ref[...].astype(F32)
     meta_ref[2:3, :] = obs_ref[0]
@@ -94,6 +102,34 @@
     meta_ref[4:5, :] = jnp.full((1, slots), pos_ref[0] // RES, jnp.int32).astype(F32)
     meta_ref[5:6, :] = jnp.full((1, slots), cnt_ref[0], jnp.int32).astype(F32)
     meta_ref[6:8, :] = jnp.zeros((2, slots), F32)
+    for send in sends:
+        send.wait()
+
+
+def table_kernel(*refs):
+    e_ref = refs[-1]
+    pairs = refs[: len(refs) - 4]
+    groups = 2 * len(pairs)
+    spot = jnp.concatenate([p[n : n + 1, :] for p in pairs for n in (4, 4 + ROWS)], 0)
+    step = jnp.concatenate([spot + F32(k) for k in range(KB)], 0).astype(jnp.int32)
+    column = lax.broadcasted_iota(jnp.int32, step.shape, 1)
+    turn = (step * column) & (SG - 1)
+    angle = turn.astype(F32) * F32(2.0 * math.pi / SG)
+    cos, sin = jnp.cos(angle) * F32(1.0 / 256.0), jnp.sin(angle) * F32(1.0 / 256.0)
+    rows = []
+    for k in range(KB):
+        c, s = cos[k * groups : (k + 1) * groups], sin[k * groups : (k + 1) * groups]
+        rows += [jnp.concatenate([c, s], 1), jnp.concatenate([-s, c], 1)]
+    table = jnp.concatenate(rows, 0)
+    high = table.astype(BF)
+    e_ref[: table.shape[0], :] = high
+    e_ref[table.shape[0] :, :] = (table - high.astype(F32)).astype(BF)
+
+
+def slot_grid(ref, k, slot, groups, rows_v):
+    real = ref[k, slot * rows_v : (slot + 1) * rows_v, :]
+    imag = ref[k, (groups + slot) * rows_v : (groups + slot + 1) * rows_v, :]
+    return jnp.concatenate([real, imag], 0)
 
 
 def expand(wu_ref, fine_index):
@@ -135,7 +171,7 @@
                     k * band : (k + 1) * band, n * RES : (n + 1) * RES
                 ]
     for s in range(groups):
-        grid = [gs_ref[k, s * 2 * rows_v : (s + 1) * 2 * rows_v, :] for k in range(KB)]
+        grid = [slot_grid(gs_ref, k, s, groups, rows_v) for k in range(KB)]
         grid = jnp.concatenate(grid, 1)
         high = grid.astype(BF)
         low = (grid - high.astype(F32)).astype(BF)
@@ -176,26 +212,36 @@
         expand(wu_ref.at[s], meta[start : start + 1, :])
         cells = dot(spread, wu_ref[s], ((1,), (1,)))
         for k in range(KB):
-            rs_ref[k, s * 2 * rows_v : (s + 1) * 2 * rows_v, :] = cells[:, k * RES : (k + 1) * RES]
+            part = cells[:, k * RES : (k + 1) * RES]
+            rs_ref[k, s * rows_v : (s + 1) * rows_v, :] = part[:rows_v]
+            rs_ref[k, (groups + s) * rows_v : (groups + s + 1) * rows_v, :] = part[rows_v:]
     for v in range(rows_v):
         rows = [rs_ref[k, pl.ds(v, band, stride=rows_v), :] for k in range(KB)]
         ct_ref[v] = jnp.concatenate(rows, 0).T.astype(BF)
     e_table = e_ref[: KB * band, :]
-    for f in range(0, RES, CHUNK):
+
+    def turn_chunk(wave, f):
+        v = wave * WAVE
         cos = tc_ref[f : f + CHUNK, :]
         sin = ts_ref[f : f + CHUNK, :]
-        for v in range(0, rows_v, WAVE):
-            cells = ct_ref[v : v + WAVE, f : f + CHUNK, :].reshape(WAVE * CHUNK, KB * band)
-            back = dot(cells, e_table, ((1,), (0,))).reshape(WAVE, CHUNK, 2 * SG)
-            real_b, imag_b = back[..., :SG], back[..., SG:]
-            m_ref[v : v + WAVE, f : f + CHUNK, :] = (real_b * cos - imag_b * sin).astype(BF)
-            m_ref[v : v + WAVE, RES + f : RES + f + CHUNK, :] = (
-                imag_b * cos + real_b * sin
-            ).astype(BF)
-    for v in range(rows_v):
+        cells = ct_ref[v : v + WAVE, f : f + CHUNK, :].reshape(WAVE * CHUNK, KB * band)
+        back = dot(cells, e_table, ((1,), (0,))).reshape(WAVE, CHUNK, 2 * SG)
+        real_b, imag_b = back[..., :SG], back[..., SG:]
+        m_ref[v : v + WAVE, f : f + CHUNK, :] = (real_b * cos - imag_b * sin).astype(BF)
+        m_ref[v : v + WAVE, RES + f : RES + f + CHUNK, :] = (
+            imag_b * cos + real_b * sin
+        ).astype(BF)
+
+    def make_block(v):
         image = dot(d_table, m_ref[v], ((1,), (0,)))
         for k in range(KB):
             im_ref[k, pl.ds(v, lines, stride=rows_v), :] = image[:, k * RES : (k + 1) * RES]
+
+    for n in range(0, RES, CHUNK):
+        for wave in range(rows_v // WAVE):
+            turn_chunk(wave, n)
+    for v in range(rows_v):
+        make_block(v)
     for k in range(KB):
         out_ref[:, k * RES : (k + 1) * RES] = im_ref[k].astype(BF)
 
@@ -206,9 +252,37 @@
     rows_v = facet_data.shape[1]
     slots = vis_u_fine.shape[1]
     facet = lax.axis_index("facet")
-    inside = jnp.arange(SG, dtype=jnp.int32)
-
-    gathered = gather_by_exchange(facet_data, "sub")
+
+    params = pltpu.CompilerParams(vmem_limit_bytes=24 * 1024 * 1024)
+    vmem = pl.BlockSpec(memory_space=pltpu.VMEM)
+    smem = pl.BlockSpec(memory_space=pltpu.SMEM)
+    hbm = pl.BlockSpec(memory_space=pltpu.HBM)
+    copies, meta = pl.pallas_call(
+        lead_kernel,
+        out_shape=(
+            jax.ShapeDtypeStruct((subs,) + facet_data.shape, BF),
+            jax.ShapeDtypeStruct((ROWS, slots), F32),
+        ),
+        in_specs=[smem] * 2 + [hbm] * 4,
+        out_specs=(hbm, vmem),
+        scratch_shapes=[
+            pltpu.VMEM(facet_data.shape, BF),
+            pltpu.VMEM((1, slots), jnp.int32),
+            pltpu.VMEM((1, slots), jnp.int32),
+            pltpu.VMEM((2, 1, slots), F32),
+            pltpu.SemaphoreType.DMA((4,)),
+            pltpu.SemaphoreType.DMA((subs,)),
+        ],
+        compiler_params=params,
+        name="lead",
+    )(
+        subgrid_pos, vis_counts,
+        *(
+            pltpu.with_memory_space_constraint(value, pltpu.HBM)
+            for value in (facet_data, vis_u_fine, vis_v_fine, vis_observed)
+        ),
+    )
+    gathered = lax.all_to_all(copies, "sub", 0, 0, tiled=True)
 
     table = block_tables(facets, subs)
     high_d, low_d = host_split(table)
@@ -219,38 +293,20 @@
     turn = np.arange(RES)[:, None] * np.arange(SG)[None, :] * (2.0 * math.pi / 65536)
     tw_cos = jnp.asarray(np.cos(turn).astype(np.float32))
     tw_sin = jnp.asarray(np.sin(turn).astype(np.float32))
-    params = pltpu.CompilerParams(vmem_limit_bytes=24 * 1024 * 1024)
-    vmem = pl.BlockSpec(memory_space=pltpu.VMEM)
-    smem = pl.BlockSpec(memory_space=pltpu.SMEM)
-    meta = pl.pallas_call(
-        pack_kernel,
-        out_shape=jax.ShapeDtypeStruct((ROWS, slots), F32),
-        in_specs=[smem] * 2 + [vmem] * 7,
-        out_specs=vmem,
-        compiler_params=params,
-        name="pack_meta",
-    )(
-        subgrid_pos, vis_counts, vis_u_fine, vis_v_fine, vis_observed,
-        into, outof, tw_cos, tw_sin,
-    )
     partner = lax.ppermute(meta, "facet", [(n, n ^ 1) for n in range(facets)])
     pairs = [jnp.concatenate([meta, partner], 0)]
     for d in range(2, facets, 2):
         ring = [(n, (n + d) % facets) for n in range(facets)]
         pairs.append(lax.ppermute(pairs[0], "facet", ring))
 
-    spot = jnp.concatenate([p[n : n + 1] for p in pairs for n in (4, 4 + ROWS)], 0)
-    spot = spot.astype(jnp.int32)
-    step = spot[None] + jnp.arange(KB, dtype=jnp.int32)[:, None, None]
-    turn = (step * inside).reshape(KB * facets, SG) % SG
-    angle = turn.astype(F32) * (2.0 * math.pi / SG)
-    scale = F32(1.0 / 256.0)
-    cos, sin = jnp.cos(angle) * scale, jnp.sin(angle) * scale
-    lines = jnp.stack(
-        [jnp.concatenate([cos, sin], 1), jnp.concatenate([-sin, cos], 1)], 1
-    ).reshape(2 * KB * facets, 2 * SG)
-    high_e, low_e = split(lines)
-    e_table = jnp.concatenate([high_e, low_e], 0)
+    e_table = pl.pallas_call(
+        table_kernel,
+        out_shape=jax.ShapeDtypeStruct((4 * KB * facets, 2 * SG), BF),
+        in_specs=[vmem] * (3 + facets // 2),
+        out_specs=vmem,
+        compiler_params=params,
+        name="position_table",
+    )(*pairs, into, tw_cos, tw_sin)
 
     at = facet.astype(jnp.int32)[None]
     part = pl.pallas_call(

time: 65.8 us -> 58.5 us (0.89)
  local copies, waits for them, and re-layouts: 6.67 us -> 0.03 us
  Pallas kernels: 8.18 us -> 9.93 us
  waiting for transfers between devices: 6.25 us -> 5.29 us
  starting transfers between devices: 14.2 us -> 13.4 us
  other arithmetic: 1.38 us -> 0.71 us
    unnamed x24 -> x9, local copies, waits for them, and re-layouts: 5.24 us -> 0.03 us
    all_to_all x1, waiting for transfers between devices: 3.44 us -> 0.58 us  [shards(): gathered = lax.all_to_all(copies, 'sub', 0, 0, tiled=True)]
    pallas_call x1 -> x2, Pallas kernels: 0.01 us -> 2.03 us  [the longest x1 1.73 us: shards(): pl.pallas_call(lead_kernel, out_shape=(jax.ShapeDtypeStruct((subs,) + fac...]
    ppermute x3, waiting for transfers between devices: 1.97 us -> 3.87 us  [shards(): pairs.append(lax.ppermute(pairs[0], 'facet', ring))]
    ppermute x3, starting transfers between devices: 5.11 us -> 3.77 us  [shards(): pairs.append(lax.ppermute(pairs[0], 'facet', ring))]
    all_to_all x1, starting transfers between devices: 7.6 us -> 8.56 us  [shards(): gathered = lax.all_to_all(copies, 'sub', 0, 0, tiled=True)]
    broadcast_in_dim x1 -> x0, local copies, waits for them, and re-layouts: 0.87 us -> none  [gather_by_exchange(): copies = jnp.broadcast_to(value[None], (count,) + value.shape)]
  transfers between devices with their start and end apart: 5 -> 5, of which waited for: 4 -> 4; matrix products, arithmetic and copies ran while one was open for 3% -> 0% of each run, Pallas kernels for 0% -> 1%
where the time goes in v2:
time: 58.5 us; the launch traced here: 57.5 us
  blocking collectives  26.2 us (45%)
  starting transfers between devices  13.4 us (23%)
  Pallas kernels  9.93 us (17%)
  waiting for transfers between devices  5.29 us (9%)
  between operations  1.99 us (3%)
  other arithmetic  0.71 us (1%)
    all_to_all x1, blocking collectives, shards(): image = lax.all_to_all(image, 'sub', 0, 0, tiled=True)  14.5 us
    all_to_all x1, blocking collectives, shards(): parts = lax.all_to_all(part, 'facet', 0, 0, tiled=True)  11.7 us
    all_to_all x1, starting transfers between devices, shards(): gathered = lax.all_to_all(copies, 'sub', 0, 0, tiled=True)  8.56 us
    pallas_call x1, Pallas kernels, shards(): pl.pallas_call(backward_kernel, out_shape=(jax.ShapeDtypeStruct((2, 1, sl...  4.37 us
    ppermute x3, waiting for transfers between devices, shards(): pairs.append(lax.ppermute(pairs[0], 'facet', ring))  3.87 us
    ppermute x3, starting transfers between devices, shards(): pairs.append(lax.ppermute(pairs[0], 'facet', ring))  3.77 us
    pallas_call x1, Pallas kernels, shards(): pl.pallas_call(forward_kernel, out_shape=jax.ShapeDtypeStruct((facets, fa...  3.53 us
    pallas_call x1, Pallas kernels, shards(): pl.pallas_call(lead_kernel, out_shape=(jax.ShapeDtypeStruct((subs,) + fac...  1.73 us
  transfers between devices with their start and end apart: 5, of which 4 were waited for; matrix products, arithmetic and copies ran while one was open for 0% of the time, Pallas kernels for 1%

profile of v2, /device:TPU:1, one launch (start us, length us, event | category | flops | bytes accessed | tf_op | source)
XLA Modules:
  0.0 57.5 jit_solution(11071280662652574612)
XLA Ops:
  1.9 1.7 %lead.1 = (bf16[16,2,16,512]{3,2,1,0:T(8,128)(2,1)}, f32[8,512]{1,0:T(8,128)S(1)}) custom-call(s32[1]{0:T(128)S(6)} %copy.13.pos_ref, s32[1]{0:T(128)S(6)} %copy.14.cnt_ref, bf16[2,16,512]{2,1,0:T(8,128)(2,1)} %y_hbm.1, s32[1,512]{1,0:T(1,128)} %u_hbm.1, s32[1,512]{1,0:T(1,128)} %v_hbm.1, f32[2,1,512]{2,1,0:T(1,128)} %obs_hbm.1), custom_call_target="tpu_custom_call" | custom-call | tf_op jit(solution)/shard_map/lead/pallas_call | solution.py:260
  3.7 0.0 copy-start
  3.7 0.0 copy-start.1
  3.7 0.0 copy-start.2
  3.7 8.6 %all-to-all-start = ((bf16[16,2,16,512]{3,2,1,0:T(8,128)(2,1)}), bf16[16,2,16,512]{3,2,1,0:T(8,128)(2,1)S(1)}, u32[]{:S(2)}, u32[]{:S(2)}) async-start(bf16[16,2,16,512]{3,2,1,0:T(8,128)(2,1)} %get-tuple-element.6), calls=%async_computation | async-start | bytes 1048576 | tf_op jit(solution)/shard_map/all_to_all | solution.py:285
  12.3 1.0 %collective-permute-start = (f32[8,512]{1,0:T(8,128)S(1)}, f32[8,512]{1,0:T(8,128)S(1)}, u32[]{:S(2)}, u32[]{:S(2)}) collective-permute-start(f32[8,512]{1,0:T(8,128)S(1)} %get-tuple-element.7), channel_id=1, source_target_pairs={{0,16},{16,0},{32,48},{48,32},{64,80},{80,64},{96,112},{112,96},{1... | collective-permute-start | bytes 49160 | tf_op jit(solution)/shard_map/ppermute | solution.py:296
  13.3 0.8 %collective-permute-done = f32[8,512]{1,0:T(8,128)S(1)} collective-permute-done((f32[8,512]{1,0:T(8,128)S(1)}, f32[8,512]{1,0:T(8,128)S(1)}, u32[]{:S(2)}, u32[]{:S(2)}) %collective-permute-start) | collective-permute-done | bytes 16416 | tf_op jit(solution)/shard_map/ppermute | solution.py:296
  14.1 2.7 %collective-permute-start.3 = (f32[16,512]{1,0:T(8,128)S(1)}, f32[16,512]{1,0:T(8,128)S(1)}, u32[]{:S(2)}, u32[]{:S(2)}) collective-permute-start(f32[16,512]{1,0:T(8,128)S(1)} %constant_dynamic-update-slice_fusion.refs_0_), channel_id=1, source_target_pairs={{0,96},{16,112},{32,0},{48,16},{64,32},{80,48},{96,64},{112,80},{1... | collective-permute-start | bytes 98312 | tf_op jit(solution)/shard_map/ppermute | solution.py:300
  16.9 0.3 collective-permute-start.2
  17.2 0.7 %collective-permute-start.1 = (f32[16,512]{1,0:T(8,128)S(1)}, f32[16,512]{1,0:T(8,128)S(1)}, u32[]{:S(2)}, u32[]{:S(2)}) collective-permute-start(f32[16,512]{1,0:T(8,128)S(1)} %constant_dynamic-update-slice_fusion.refs_0_), channel_id=1, source_target_pairs={{0,32},{16,48},{32,64},{48,80},{64,96},{80,112},{96,0},{112,16},{1... | collective-permute-start | bytes 98312 | tf_op jit(solution)/shard_map/ppermute | solution.py:300
  17.9 0.0 collective-permute-done.3.refs_3_
  17.9 3.5 %collective-permute-done.2.refs_2_ = f32[16,512]{1,0:T(8,128)S(1)} collective-permute-done((f32[16,512]{1,0:T(8,128)S(1)}, f32[16,512]{1,0:T(8,128)S(1)}, u32[]{:S(2)}, u32[]{:S(2)}) %collective-permute-start.2) | collective-permute-done | bytes 32800 | tf_op jit(solution)/shard_map/ppermute | solution.py:300
  21.4 0.4 collective-permute-done.1.refs_1_
  21.8 0.0 copy-done
  21.8 0.0 copy-done.1
  21.8 0.0 copy-done.2
  21.8 0.3 position_table.1.e_ref
  22.1 0.6 %all-to-all-done = bf16[16,2,16,512]{3,2,1,0:T(8,128)(2,1)S(1)} async-done(((bf16[16,2,16,512]{3,2,1,0:T(8,128)(2,1)}), bf16[16,2,16,512]{3,2,1,0:T(8,128)(2,1)S(1)}, u32[]{:S(2)}, u32[]{:S(2)}) %all-to-all-start) | async-done | bytes 524320 | tf_op jit(solution)/shard_map/all_to_all | solution.py:285
  22.7 3.5 %forward_share.1 = bf16[8,8,2,512]{3,2,1,0:T(2,128)(2,1)S(1)} custom-call(s32[1]{0:T(128)} %bitcast.at_ref, bf16[512,512]{1,0:T(8,128)(2,1)S(1)} %bitcast.3, bf16[8,256,64]{2,1,0:T(8,128)(2,1)S(1)} %copy-done.2, f32[128,512]{1,0:T(8,128)S(1)} %copy-done.1, f32[128,512]{1,0:T(8,128)S(1)} %copy-done, bf16[128,1024]{1,0:T(8,128)(2,1)S(1)} %position_table.1.e_ref, ...), custom_call_target="tpu_custom_call" | custom-call | tf_op jit(solution)/shard_map/forward_share/pallas_call | solution.py:312
  26.2 0.0 copy-start.3
  26.2 11.7 %all_to_all.15.part_ref = bf16[8,8,2,512]{3,2,1,0:T(2,128)(2,1)S(1)} all-to-all(bf16[8,8,2,512]{3,2,1,0:T(2,128)(2,1)S(1)} %forward_share.1), channel_id=1, replica_groups=mesh['facet'=8,'sub'=16] {'facet'}, dimensions={0} | all-to-all | bytes 262144 | tf_op jit(solution)/shard_map/all_to_all | solution.py:328
  37.9 4.4 %backward_share.1 = (f32[2,1,512]{2,1,0:T(1,128)}, bf16[512,512]{1,0:T(8,128)(2,1)S(1)}) custom-call(s32[1]{0:T(128)} %bitcast.at_ref, bf16[8,8,2,512]{3,2,1,0:T(2,128)(2,1)S(1)} %all_to_all.15.part_ref, bf16[128,1024]{1,0:T(8,128)(2,1)S(1)} %position_table.1.e_ref, f32[128,512]{1,0:T(8,128)S(1)} %copy-done.1, f32[128,512]{1,0:T(8,128)S(1)} %copy-done, ...), custom_call_target="tpu_custom_call" | custom-call | tf_op jit(solution)/shard_map/backward_share/pallas_call | solution.py:330
  42.3 14.5 %all_to_all.16 = bf16[16,2,16,512]{3,2,1,0:T(8,128)(2,1)S(1)} all-to-all(bf16[16,2,16,512]{3,2,1,0:T(8,128)(2,1)S(1)} %bitcast.4), channel_id=1, replica_groups=mesh['facet'=8,'sub'=16] {'sub'}, dimensions={0} | all-to-all | bytes 1048576 | tf_op jit(solution)/shard_map/all_to_all | solution.py:350
  56.8 0.7 %convert_reduce_fusion = f32[2,16,512]{2,1,0:T(8,128)} fusion(bf16[16,2,16,512]{3,2,1,0:T(8,128)(2,1)S(1)} %all_to_all.16), kind=kLoop, calls=%fused_computation | loop fusion | flops 507904 | bytes 589824 | tf_op jit(solution)/shard_map/reduce_sum | solution.py:351
  (3 shorter events, 0.0 us)
Async XLA Ops:
  3.7 18.1 %copy-start = (f32[128,512]{1,0:T(8,128)S(1)}, f32[128,512]{1,0:T(8,128)}, u32[]{:S(2)}) copy-start(f32[128,512]{1,0:T(8,128)} %constant.19.clone.refs_6_.ts_ref) | copy-start | bytes 786436
  3.7 18.1 %copy-start.1 = (f32[128,512]{1,0:T(8,128)S(1)}, f32[128,512]{1,0:T(8,128)}, u32[]{:S(2)}) copy-start(f32[128,512]{1,0:T(8,128)} %constant.18.clone.refs_5_.tc_ref) | copy-start | bytes 786436
  3.7 18.1 %copy-start.2 = (bf16[8,256,64]{2,1,0:T(8,128)(2,1)S(1)}, bf16[8,256,64]{2,1,0:T(8,128)(2,1)}, u32[]{:S(2)}) copy-start(bf16[8,256,64]{2,1,0:T(8,128)(2,1)} %constant.16.clone.refs_4_.d_ref) | copy-start | bytes 786436
  3.7 19.0 %all-to-all-start = ((bf16[16,2,16,512]{3,2,1,0:T(8,128)(2,1)}), bf16[16,2,16,512]{3,2,1,0:T(8,128)(2,1)S(1)}, u32[]{:S(2)}, u32[]{:S(2)}) async-start(bf16[16,2,16,512]{3,2,1,0:T(8,128)(2,1)} %get-tuple-element.6), calls=%async_computation | async-start | bytes 1048576 | tf_op jit(solution)/shard_map/all_to_all | solution.py:285
  12.3 1.9 %collective-permute-start = (f32[8,512]{1,0:T(8,128)S(1)}, f32[8,512]{1,0:T(8,128)S(1)}, u32[]{:S(2)}, u32[]{:S(2)}) collective-permute-start(f32[8,512]{1,0:T(8,128)S(1)} %get-tuple-element.7), channel_id=1, source_target_pairs={{0,16},{16,0},{32,48},{48,32},{64,80},{80,64},{96,112},{112,96},{1... | collective-permute-start | bytes 49160 | tf_op jit(solution)/shard_map/ppermute | solution.py:296
  14.1 3.8 %collective-permute-start.3 = (f32[16,512]{1,0:T(8,128)S(1)}, f32[16,512]{1,0:T(8,128)S(1)}, u32[]{:S(2)}, u32[]{:S(2)}) collective-permute-start(f32[16,512]{1,0:T(8,128)S(1)} %constant_dynamic-update-slice_fusion.refs_0_), channel_id=1, source_target_pairs={{0,96},{16,112},{32,0},{48,16},{64,32},{80,48},{96,64},{112,80},{1... | collective-permute-start | bytes 98312 | tf_op jit(solution)/shard_map/ppermute | solution.py:300
  16.9 4.6 %collective-permute-start.2 = (f32[16,512]{1,0:T(8,128)S(1)}, f32[16,512]{1,0:T(8,128)S(1)}, u32[]{:S(2)}, u32[]{:S(2)}) collective-permute-start(f32[16,512]{1,0:T(8,128)S(1)} %constant_dynamic-update-slice_fusion.refs_0_), channel_id=1, source_target_pairs={{0,64},{16,80},{32,96},{48,112},{64,0},{80,16},{96,32},{112,48},{1... | collective-permute-start | bytes 98312 | tf_op jit(solution)/shard_map/ppermute | solution.py:300
  17.2 4.6 %collective-permute-start.1 = (f32[16,512]{1,0:T(8,128)S(1)}, f32[16,512]{1,0:T(8,128)S(1)}, u32[]{:S(2)}, u32[]{:S(2)}) collective-permute-start(f32[16,512]{1,0:T(8,128)S(1)} %constant_dynamic-update-slice_fusion.refs_0_), channel_id=1, source_target_pairs={{0,32},{16,48},{32,64},{48,80},{64,96},{80,112},{96,0},{112,16},{1... | collective-permute-start | bytes 98312 | tf_op jit(solution)/shard_map/ppermute | solution.py:300
  26.2 11.7 %copy-start.3 = (bf16[8,32,256]{2,1,0:T(8,128)(2,1)S(1)}, bf16[8,32,256]{2,1,0:T(8,128)(2,1)}, u32[]{:S(2)}) copy-start(bf16[8,32,256]{2,1,0:T(8,128)(2,1)} %constant.17.clone.d_ref) | copy-start | bytes 393220

commit v3 on v2

--- a/solution.py
+++ b/solution.py
@@ -15,7 +15,7 @@
 KB = SG // RES
 BATCH = 4
 CHUNK = 16
-WAVE = 4
+WAVE = 16
 SUB = 8
 ROWS = 8
 BF = jnp.bfloat16
@@ -78,11 +78,10 @@
     y_ref, u_ref, v_ref, obs_ref, load_sem, send_sem,
 ):
     slots = u_ref.shape[1]
+    pairs = [(y_hbm, y_ref), (u_hbm, u_ref), (v_hbm, v_ref), (obs_hbm, obs_ref)]
     loads = [
         pltpu.make_async_copy(source, target, load_sem.at[n])
-        for n, (source, target) in enumerate(
-            [(y_hbm, y_ref), (u_hbm, u_ref), (v_hbm, v_ref), (obs_hbm, obs_ref)]
-        )
+        for n, (source, target) in enumerate(pairs)
     ]
     for load in loads:
         load.start()
@@ -106,6 +105,13 @@
         send.wait()
 
 
+def interleave(real, imag):
+    parts = []
+    for n in range(0, real.shape[1], RES):
+        parts += [real[:, n : n + RES], imag[:, n : n + RES]]
+    return jnp.concatenate(parts, 1)
+
+
 def table_kernel(*refs):
     e_ref = refs[-1]
     pairs = refs[: len(refs) - 4]
@@ -119,7 +125,7 @@
     rows = []
     for k in range(KB):
         c, s = cos[k * groups : (k + 1) * groups], sin[k * groups : (k + 1) * groups]
-        rows += [jnp.concatenate([c, s], 1), jnp.concatenate([-s, c], 1)]
+        rows += [interleave(c, s), interleave(-s, c)]
     table = jnp.concatenate(rows, 0)
     high = table.astype(BF)
     e_ref[: table.shape[0], :] = high
@@ -138,11 +144,12 @@
         wu_ref[n * KS : (n + 2) * KS, :] = jnp.concatenate(rows[n : n + 2], 0).astype(BF)
 
 
-def forward_kernel(at_ref, y_ref, d_ref, tc_ref, ts_ref, e_ref, *refs):
+def forward_kernel(y_ref, d_ref, tc_ref, ts_ref, e_ref, *refs):
     meta_refs = refs[:-4]
     part_ref, ys_ref, gs_ref, wu_ref = refs[-4:]
     groups = 2 * len(meta_refs)
-    d_table = d_ref[at_ref[0]]
+    at = lax.axis_index("facet")
+    d_table = d_ref[at]
     pieces = y_ref.shape[0]
     half = e_ref.shape[0] // 2
     band = half // KB
@@ -162,7 +169,7 @@
             sin = ts_ref[...].reshape(RES // SUB, SUB, SG)
             real_h = (real_g * cos + imag_g * sin).reshape(RES, SG).astype(BF)
             imag_h = (imag_g * cos - real_g * sin).reshape(RES, SG).astype(BF)
-            turned.append(jnp.concatenate([real_h, imag_h], 1))
+            turned.append(interleave(real_h, imag_h))
         share = dot(e_ref[...], jnp.concatenate(turned, 0), ((1,), (1,)))
         share = share[:half] + share[half:]
         for n in range(BATCH):
@@ -182,31 +189,34 @@
         wv = weights(meta[start + 1 : start + 2, :], rows_v)
         real = jnp.sum(along[:rows_v] * wv, 0, keepdims=True)
         imag = jnp.sum(along[rows_v:] * wv, 0, keepdims=True)
-        place = slot_place(at_ref[0], s, groups)
+        place = slot_place(at, s, groups)
         both = jnp.concatenate([real, imag], 0).astype(BF)
         for n in range(groups):
             part_ref[n, place] = both
 
 
-def backward_kernel(at_ref, part_ref, e_ref, tc_ref, ts_ref, d_ref, *refs):
-    meta_refs = refs[:-8]
-    res_ref, out_ref, pred_ref, rs_ref, im_ref, wu_ref, ct_ref, m_ref = refs[-8:]
+def backward_kernel(part_ref, e_ref, tc_ref, ts_ref, d_ref, *refs):
+    meta_refs = refs[:-10]
+    res_hbm, out_ref, pred_ref, rs_ref, im_ref, wu_ref, ct_ref, m_ref, res_ref, sem = refs[-10:]
     groups = 2 * len(meta_refs)
     slots = res_ref.shape[2]
-    d_table = d_ref[at_ref[0]]
+    store = pltpu.make_async_copy(res_ref, res_hbm, sem)
+    at = lax.axis_index("facet")
+    d_table = d_ref[at]
     lines = d_table.shape[0]
     band = 2 * groups
     rows_v = rs_ref.shape[1] // band
     pred_ref[...] = jnp.sum(part_ref[...].astype(F32), 0)
     slot = lax.broadcasted_iota(jnp.int32, (2, slots), 1).astype(F32)
     for s in range(groups):
-        place = slot_place(at_ref[0], s, groups)
+        place = slot_place(at, s, groups)
         meta, start = slot_rows(meta_refs, s)
         seen = meta[start + 2 : start + 4, :] - pred_ref[place]
         residual = jnp.where(slot < meta[start + 5 : start + 6, :], seen, F32(0.0))
         if s == 0:
             res_ref[0] = residual[0:1]
             res_ref[1] = residual[1:2]
+            store.start()
         wv = weights(meta[start + 1 : start + 2, :], rows_v)
         spread = jnp.concatenate([wv * residual[0:1], wv * residual[1:2]], 0).astype(BF)
         expand(wu_ref.at[s], meta[start : start + 1, :])
@@ -218,19 +228,22 @@
     for v in range(rows_v):
         rows = [rs_ref[k, pl.ds(v, band, stride=rows_v), :] for k in range(KB)]
         ct_ref[v] = jnp.concatenate(rows, 0).T.astype(BF)
-    e_table = e_ref[: KB * band, :]
 
     def turn_chunk(wave, f):
         v = wave * WAVE
-        cos = tc_ref[f : f + CHUNK, :]
-        sin = ts_ref[f : f + CHUNK, :]
         cells = ct_ref[v : v + WAVE, f : f + CHUNK, :].reshape(WAVE * CHUNK, KB * band)
-        back = dot(cells, e_table, ((1,), (0,))).reshape(WAVE, CHUNK, 2 * SG)
-        real_b, imag_b = back[..., :SG], back[..., SG:]
-        m_ref[v : v + WAVE, f : f + CHUNK, :] = (real_b * cos - imag_b * sin).astype(BF)
-        m_ref[v : v + WAVE, RES + f : RES + f + CHUNK, :] = (
-            imag_b * cos + real_b * sin
-        ).astype(BF)
+        for n in range(0, SG, RES):
+            cos = tc_ref[f : f + CHUNK, n : n + RES]
+            sin = ts_ref[f : f + CHUNK, n : n + RES]
+            back = dot(cells, e_ref[: KB * band, 2 * n : 2 * (n + RES)], ((1,), (0,)))
+            back = back.reshape(WAVE, CHUNK, 2 * RES)
+            real_b, imag_b = back[..., :RES], back[..., RES:]
+            m_ref[v : v + WAVE, f : f + CHUNK, n : n + RES] = (
+                real_b * cos - imag_b * sin
+            ).astype(BF)
+            m_ref[v : v + WAVE, RES + f : RES + f + CHUNK, n : n + RES] = (
+                imag_b * cos + real_b * sin
+            ).astype(BF)
 
     def make_block(v):
         image = dot(d_table, m_ref[v], ((1,), (0,)))
@@ -244,6 +257,7 @@
         make_block(v)
     for k in range(KB):
         out_ref[:, k * RES : (k + 1) * RES] = im_ref[k].astype(BF)
+    store.wait()
 
 
 def shards(facet_data, subgrid_pos, vis_counts, vis_u_fine, vis_v_fine, vis_observed):
@@ -251,12 +265,11 @@
     subs = lax.axis_size("sub")
     rows_v = facet_data.shape[1]
     slots = vis_u_fine.shape[1]
-    facet = lax.axis_index("facet")
 
     params = pltpu.CompilerParams(vmem_limit_bytes=24 * 1024 * 1024)
     vmem = pl.BlockSpec(memory_space=pltpu.VMEM)
+    hbm = pl.BlockSpec(memory_space=pltpu.HBM)
     smem = pl.BlockSpec(memory_space=pltpu.SMEM)
-    hbm = pl.BlockSpec(memory_space=pltpu.HBM)
     copies, meta = pl.pallas_call(
         lead_kernel,
         out_shape=(
@@ -308,11 +321,10 @@
         name="position_table",
     )(*pairs, into, tw_cos, tw_sin)
 
-    at = facet.astype(jnp.int32)[None]
     part = pl.pallas_call(
         forward_kernel,
         out_shape=jax.ShapeDtypeStruct((facets, facets, 2, slots), BF),
-        in_specs=[smem] + [vmem] * (5 + facets // 2),
+        in_specs=[vmem] * (5 + facets // 2),
         scratch_shapes=[
             pltpu.VMEM((KB, 2 * subs * rows_v, RES), F32),
             pltpu.VMEM((KB, 2 * facets * rows_v, RES), F32),
@@ -321,7 +333,7 @@
         compiler_params=params,
         name="forward_share",
     )(
-        at, gathered.reshape(2 * subs * rows_v, SG), into, tw_cos, tw_sin, e_table,
+        gathered.reshape(2 * subs * rows_v, SG), into, tw_cos, tw_sin, e_table,
         *pairs,
     )
 
@@ -333,7 +345,7 @@
             jax.ShapeDtypeStruct((2, 1, slots), F32),
             jax.ShapeDtypeStruct((2 * subs * rows_v, SG), BF),
         ),
-        in_specs=[smem] + [vmem] * (5 + facets // 2),
+        in_specs=[vmem] * (5 + facets // 2),
         scratch_shapes=[
             pltpu.VMEM((facets, 2, slots), F32),
             pltpu.VMEM((KB, 2 * facets * rows_v, RES), F32),
@@ -341,10 +353,13 @@
             pltpu.VMEM((facets, SG, slots), BF),
             pltpu.VMEM((rows_v, RES, 2 * KB * facets), BF),
             pltpu.VMEM((rows_v, 2 * RES, SG), BF),
+            pltpu.VMEM((2, 1, slots), F32),
+            pltpu.SemaphoreType.DMA(()),
         ],
+        out_specs=(hbm, vmem),
         compiler_params=params,
         name="backward_share",
-    )(at, parts, e_table, tw_cos, tw_sin, outof, *pairs)
+    )(parts, e_table, tw_cos, tw_sin, outof, *pairs)
 
     image = image.reshape(subs, 2, rows_v, SG)
     image = lax.all_to_all(image, "sub", 0, 0, tiled=True)

time: 58.5 us -> 58.4 us (level)
  no operation moved by 1% of the time
where the time goes in v3:
time: 58.4 us; the launch traced here: 57.5 us
  blocking collectives  26.2 us (45%)
  starting transfers between devices  13.4 us (23%)
  Pallas kernels  9.87 us (17%)
  waiting for transfers between devices  5.29 us (9%)
  between operations  2 us (3%)
  other arithmetic  0.71 us (1%)
    all_to_all x1, blocking collectives, shards(): image = lax.all_to_all(image, 'sub', 0, 0, tiled=True)  14.5 us
    all_to_all x1, blocking collectives, shards(): parts = lax.all_to_all(part, 'facet', 0, 0, tiled=True)  11.7 us
    all_to_all x1, starting transfers between devices, shards(): gathered = lax.all_to_all(copies, 'sub', 0, 0, tiled=True)  8.56 us
    pallas_call x1, Pallas kernels, shards(): pl.pallas_call(backward_kernel, out_shape=(jax.ShapeDtypeStruct((2, 1, sl...  4.46 us
    ppermute x3, waiting for transfers between devices, shards(): pairs.append(lax.ppermute(pairs[0], 'facet', ring))  3.87 us
    ppermute x3, starting transfers between devices, shards(): pairs.append(lax.ppermute(pairs[0], 'facet', ring))  3.77 us
    pallas_call x1, Pallas kernels, shards(): pl.pallas_call(forward_kernel, out_shape=jax.ShapeDtypeStruct((facets, fa...  3.37 us
    pallas_call x1, Pallas kernels, shards(): pl.pallas_call(lead_kernel, out_shape=(jax.ShapeDtypeStruct((subs,) + fac...  1.73 us
  transfers between devices with their start and end apart: 5, of which 4 were waited for; matrix products, arithmetic and copies ran while one was open for 0% of the time, Pallas kernels for 1%

profile of v3, /device:TPU:1, one launch (start us, length us, event | category | flops | bytes accessed | tf_op | source)
XLA Modules:
  0.0 57.5 jit_solution(13495508353761525706)
XLA Ops:
  1.9 1.7 %lead.1 = (bf16[16,2,16,512]{3,2,1,0:T(8,128)(2,1)}, f32[8,512]{1,0:T(8,128)S(1)}) custom-call(s32[1]{0:T(128)S(6)} %copy.13.pos_ref, s32[1]{0:T(128)S(6)} %copy.14.cnt_ref, bf16[2,16,512]{2,1,0:T(8,128)(2,1)} %y_hbm.1, s32[1,512]{1,0:T(1,128)} %u_hbm.1, s32[1,512]{1,0:T(1,128)} %v_hbm.1, f32[2,1,512]{2,1,0:T(1,128)} %obs_hbm.1), custom_call_target="tpu_custom_call" | custom-call | tf_op jit(solution)/shard_map/lead/pallas_call | solution.py:273
  3.7 0.0 copy-start
  3.7 0.0 copy-start.1
  3.7 0.0 copy-start.2
  3.7 8.6 %all-to-all-start = ((bf16[16,2,16,512]{3,2,1,0:T(8,128)(2,1)}), bf16[16,2,16,512]{3,2,1,0:T(8,128)(2,1)S(1)}, u32[]{:S(2)}, u32[]{:S(2)}) async-start(bf16[16,2,16,512]{3,2,1,0:T(8,128)(2,1)} %get-tuple-element.6), calls=%async_computation | async-start | bytes 1048576 | tf_op jit(solution)/shard_map/all_to_all | solution.py:298
  12.3 1.0 %collective-permute-start = (f32[8,512]{1,0:T(8,128)S(1)}, f32[8,512]{1,0:T(8,128)S(1)}, u32[]{:S(2)}, u32[]{:S(2)}) collective-permute-start(f32[8,512]{1,0:T(8,128)S(1)} %get-tuple-element.7), channel_id=1, source_target_pairs={{0,16},{16,0},{32,48},{48,32},{64,80},{80,64},{96,112},{112,96},{1... | collective-permute-start | bytes 49160 | tf_op jit(solution)/shard_map/ppermute | solution.py:309
  13.3 0.8 %collective-permute-done = f32[8,512]{1,0:T(8,128)S(1)} collective-permute-done((f32[8,512]{1,0:T(8,128)S(1)}, f32[8,512]{1,0:T(8,128)S(1)}, u32[]{:S(2)}, u32[]{:S(2)}) %collective-permute-start) | collective-permute-done | bytes 16416 | tf_op jit(solution)/shard_map/ppermute | solution.py:309
  14.1 2.7 %collective-permute-start.3 = (f32[16,512]{1,0:T(8,128)S(1)}, f32[16,512]{1,0:T(8,128)S(1)}, u32[]{:S(2)}, u32[]{:S(2)}) collective-permute-start(f32[16,512]{1,0:T(8,128)S(1)} %constant_dynamic-update-slice_fusion.refs_0_), channel_id=1, source_target_pairs={{0,96},{16,112},{32,0},{48,16},{64,32},{80,48},{96,64},{112,80},{1... | collective-permute-start | bytes 98312 | tf_op jit(solution)/shard_map/ppermute | solution.py:313
  16.9 0.3 collective-permute-start.2
  17.2 0.7 %collective-permute-start.1 = (f32[16,512]{1,0:T(8,128)S(1)}, f32[16,512]{1,0:T(8,128)S(1)}, u32[]{:S(2)}, u32[]{:S(2)}) collective-permute-start(f32[16,512]{1,0:T(8,128)S(1)} %constant_dynamic-update-slice_fusion.refs_0_), channel_id=1, source_target_pairs={{0,32},{16,48},{32,64},{48,80},{64,96},{80,112},{96,0},{112,16},{1... | collective-permute-start | bytes 98312 | tf_op jit(solution)/shard_map/ppermute | solution.py:313
  17.9 0.0 collective-permute-done.3.refs_3_
  17.9 3.5 %collective-permute-done.2.refs_2_ = f32[16,512]{1,0:T(8,128)S(1)} collective-permute-done((f32[16,512]{1,0:T(8,128)S(1)}, f32[16,512]{1,0:T(8,128)S(1)}, u32[]{:S(2)}, u32[]{:S(2)}) %collective-permute-start.2) | collective-permute-done | bytes 32800 | tf_op jit(solution)/shard_map/ppermute | solution.py:313
  21.4 0.4 collective-permute-done.1.refs_1_
  21.8 0.0 copy-done
  21.8 0.0 copy-done.1
  21.8 0.0 copy-done.2
  21.8 0.3 position_table.1.e_ref
  22.1 0.6 %all-to-all-done = bf16[16,2,16,512]{3,2,1,0:T(8,128)(2,1)S(1)} async-done(((bf16[16,2,16,512]{3,2,1,0:T(8,128)(2,1)}), bf16[16,2,16,512]{3,2,1,0:T(8,128)(2,1)S(1)}, u32[]{:S(2)}, u32[]{:S(2)}) %all-to-all-start) | async-done | bytes 524320 | tf_op jit(solution)/shard_map/all_to_all | solution.py:298
  22.7 3.4 %forward_share.1 = bf16[8,8,2,512]{3,2,1,0:T(2,128)(2,1)S(1)} custom-call(bf16[512,512]{1,0:T(8,128)(2,1)S(1)} %bitcast.2, bf16[8,256,64]{2,1,0:T(8,128)(2,1)S(1)} %copy-done.2, f32[128,512]{1,0:T(8,128)S(1)} %copy-done.1, f32[128,512]{1,0:T(8,128)S(1)} %copy-done, bf16[128,1024]{1,0:T(8,128)(2,1)S(1)} %position_table.1.e_ref, ...), custom_call_target="tpu_custom_call" | custom-call | tf_op jit(solution)/shard_map/forward_share/pallas_call | solution.py:324
  26.1 0.0 copy-start.3
  26.1 11.7 %all_to_all.15.part_ref = bf16[8,8,2,512]{3,2,1,0:T(2,128)(2,1)S(1)} all-to-all(bf16[8,8,2,512]{3,2,1,0:T(2,128)(2,1)S(1)} %forward_share.1), channel_id=1, replica_groups=mesh['facet'=8,'sub'=16] {'facet'}, dimensions={0} | all-to-all | bytes 262144 | tf_op jit(solution)/shard_map/all_to_all | solution.py:340
  37.8 4.5 %backward_share.1 = (f32[2,1,512]{2,1,0:T(1,128)}, bf16[512,512]{1,0:T(8,128)(2,1)S(1)}) custom-call(bf16[8,8,2,512]{3,2,1,0:T(2,128)(2,1)S(1)} %all_to_all.15.part_ref, bf16[128,1024]{1,0:T(8,128)(2,1)S(1)} %position_table.1.e_ref, f32[128,512]{1,0:T(8,128)S(1)} %copy-done.1, f32[128,512]{1,0:T(8,128)S(1)} %copy-done, bf16[8,32,256]{2,1,0:T(8,128)(2,1)S(1)} %copy-done.3, ...), custom_call_target="tpu_custom_call" | custom-call | tf_op jit(solution)/shard_map/backward_share/pallas_call | solution.py:342
  42.3 14.5 %all_to_all.16 = bf16[16,2,16,512]{3,2,1,0:T(8,128)(2,1)S(1)} all-to-all(bf16[16,2,16,512]{3,2,1,0:T(8,128)(2,1)S(1)} %bitcast.3), channel_id=1, replica_groups=mesh['facet'=8,'sub'=16] {'sub'}, dimensions={0} | all-to-all | bytes 1048576 | tf_op jit(solution)/shard_map/all_to_all | solution.py:365
  56.8 0.7 %convert_reduce_fusion = f32[2,16,512]{2,1,0:T(8,128)} fusion(bf16[16,2,16,512]{3,2,1,0:T(8,128)(2,1)S(1)} %all_to_all.16), kind=kLoop, calls=%fused_computation | loop fusion | flops 507904 | bytes 589824 | tf_op jit(solution)/shard_map/reduce_sum | solution.py:366
  (3 shorter events, 0.0 us)
Async XLA Ops:
  3.7 18.1 %copy-start = (f32[128,512]{1,0:T(8,128)S(1)}, f32[128,512]{1,0:T(8,128)}, u32[]{:S(2)}) copy-start(f32[128,512]{1,0:T(8,128)} %constant.13.clone.refs_6_.ts_ref) | copy-start | bytes 786436
  3.7 18.1 %copy-start.1 = (f32[128,512]{1,0:T(8,128)S(1)}, f32[128,512]{1,0:T(8,128)}, u32[]{:S(2)}) copy-start(f32[128,512]{1,0:T(8,128)} %constant.12.clone.refs_5_.tc_ref) | copy-start | bytes 786436
  3.7 18.1 %copy-start.2 = (bf16[8,256,64]{2,1,0:T(8,128)(2,1)S(1)}, bf16[8,256,64]{2,1,0:T(8,128)(2,1)}, u32[]{:S(2)}) copy-start(bf16[8,256,64]{2,1,0:T(8,128)(2,1)} %constant.10.clone.refs_4_.d_ref) | copy-start | bytes 786436
  3.7 19.0 %all-to-all-start = ((bf16[16,2,16,512]{3,2,1,0:T(8,128)(2,1)}), bf16[16,2,16,512]{3,2,1,0:T(8,128)(2,1)S(1)}, u32[]{:S(2)}, u32[]{:S(2)}) async-start(bf16[16,2,16,512]{3,2,1,0:T(8,128)(2,1)} %get-tuple-element.6), calls=%async_computation | async-start | bytes 1048576 | tf_op jit(solution)/shard_map/all_to_all | solution.py:298
  12.3 1.9 %collective-permute-start = (f32[8,512]{1,0:T(8,128)S(1)}, f32[8,512]{1,0:T(8,128)S(1)}, u32[]{:S(2)}, u32[]{:S(2)}) collective-permute-start(f32[8,512]{1,0:T(8,128)S(1)} %get-tuple-element.7), channel_id=1, source_target_pairs={{0,16},{16,0},{32,48},{48,32},{64,80},{80,64},{96,112},{112,96},{1... | collective-permute-start | bytes 49160 | tf_op jit(solution)/shard_map/ppermute | solution.py:309
  14.1 3.8 %collective-permute-start.3 = (f32[16,512]{1,0:T(8,128)S(1)}, f32[16,512]{1,0:T(8,128)S(1)}, u32[]{:S(2)}, u32[]{:S(2)}) collective-permute-start(f32[16,512]{1,0:T(8,128)S(1)} %constant_dynamic-update-slice_fusion.refs_0_), channel_id=1, source_target_pairs={{0,96},{16,112},{32,0},{48,16},{64,32},{80,48},{96,64},{112,80},{1... | collective-permute-start | bytes 98312 | tf_op jit(solution)/shard_map/ppermute | solution.py:313
  16.9 4.6 %collective-permute-start.2 = (f32[16,512]{1,0:T(8,128)S(1)}, f32[16,512]{1,0:T(8,128)S(1)}, u32[]{:S(2)}, u32[]{:S(2)}) collective-permute-start(f32[16,512]{1,0:T(8,128)S(1)} %constant_dynamic-update-slice_fusion.refs_0_), channel_id=1, source_target_pairs={{0,64},{16,80},{32,96},{48,112},{64,0},{80,16},{96,32},{112,48},{1... | collective-permute-start | bytes 98312 | tf_op jit(solution)/shard_map/ppermute | solution.py:313
  17.2 4.6 %collective-permute-start.1 = (f32[16,512]{1,0:T(8,128)S(1)}, f32[16,512]{1,0:T(8,128)S(1)}, u32[]{:S(2)}, u32[]{:S(2)}) collective-permute-start(f32[16,512]{1,0:T(8,128)S(1)} %constant_dynamic-update-slice_fusion.refs_0_), channel_id=1, source_target_pairs={{0,32},{16,48},{32,64},{48,80},{64,96},{80,112},{96,0},{112,16},{1... | collective-permute-start | bytes 98312 | tf_op jit(solution)/shard_map/ppermute | solution.py:313
  26.1 11.7 %copy-start.3 = (bf16[8,32,256]{2,1,0:T(8,128)(2,1)S(1)}, bf16[8,32,256]{2,1,0:T(8,128)(2,1)}, u32[]{:S(2)}) copy-start(bf16[8,32,256]{2,1,0:T(8,128)(2,1)} %constant.11.clone.d_ref) | copy-start | bytes 393220

commit v4 on v3

--- a/solution.py
+++ b/solution.py
@@ -15,7 +15,7 @@
 KB = SG // RES
 BATCH = 4
 CHUNK = 16
-WAVE = 16
+WAVE = 8
 SUB = 8
 ROWS = 8
 BF = jnp.bfloat16
@@ -250,11 +250,15 @@
         for k in range(KB):
             im_ref[k, pl.ds(v, lines, stride=rows_v), :] = image[:, k * RES : (k + 1) * RES]
 
-    for n in range(0, RES, CHUNK):
-        for wave in range(rows_v // WAVE):
-            turn_chunk(wave, n)
-    for v in range(rows_v):
-        make_block(v)
+    waves = rows_v // WAVE
+    steps = RES // CHUNK
+    for wave in range(waves + 1):
+        for n in range(steps):
+            if wave < waves:
+                turn_chunk(wave, n * CHUNK)
+            if wave > 0:
+                for v in range(n * WAVE // steps, (n + 1) * WAVE // steps):
+                    make_block((wave - 1) * WAVE + v)
     for k in range(KB):
         out_ref[:, k * RES : (k + 1) * RES] = im_ref[k].astype(BF)
     store.wait()

time: 58.4 us -> 58.3 us (level)
  no operation moved by 1% of the time
where the time goes in v4:
time: 58.3 us; the launch traced here: 57.3 us
  blocking collectives  26.2 us (45%)
  starting transfers between devices  13.4 us (23%)
  Pallas kernels  9.72 us (17%)
  waiting for transfers between devices  5.29 us (9%)
  between operations  2 us (3%)
  other arithmetic  0.71 us (1%)
    all_to_all x1, blocking collectives, shards(): image = lax.all_to_all(image, 'sub', 0, 0, tiled=True)  14.5 us
    all_to_all x1, blocking collectives, shards(): parts = lax.all_to_all(part, 'facet', 0, 0, tiled=True)  11.7 us
    all_to_all x1, starting transfers between devices, shards(): gathered = lax.all_to_all(copies, 'sub', 0, 0, tiled=True)  8.56 us
    pallas_call x1, Pallas kernels, shards(): pl.pallas_call(backward_kernel, out_shape=(jax.ShapeDtypeStruct((2, 1, sl...  4.31 us
    ppermute x3, waiting for transfers between devices, shards(): pairs.append(lax.ppermute(pairs[0], 'facet', ring))  3.87 us
    ppermute x3, starting transfers between devices, shards(): pairs.append(lax.ppermute(pairs[0], 'facet', ring))  3.77 us
    pallas_call x1, Pallas kernels, shards(): pl.pallas_call(forward_kernel, out_shape=jax.ShapeDtypeStruct((facets, fa...  3.37 us
    pallas_call x1, Pallas kernels, shards(): pl.pallas_call(lead_kernel, out_shape=(jax.ShapeDtypeStruct((subs,) + fac...  1.73 us
  transfers between devices with their start and end apart: 5, of which 4 were waited for; matrix products, arithmetic and copies ran while one was open for 0% of the time, Pallas kernels for 1%

profile of v4, /device:TPU:1, one launch (start us, length us, event | category | flops | bytes accessed | tf_op | source)
XLA Modules:
  0.0 57.3 jit_solution(16142712687415191407)
XLA Ops:
  1.9 1.7 %lead.1 = (bf16[16,2,16,512]{3,2,1,0:T(8,128)(2,1)}, f32[8,512]{1,0:T(8,128)S(1)}) custom-call(s32[1]{0:T(128)S(6)} %copy.13.pos_ref, s32[1]{0:T(128)S(6)} %copy.14.cnt_ref, bf16[2,16,512]{2,1,0:T(8,128)(2,1)} %y_hbm.1, s32[1,512]{1,0:T(1,128)} %u_hbm.1, s32[1,512]{1,0:T(1,128)} %v_hbm.1, f32[2,1,512]{2,1,0:T(1,128)} %obs_hbm.1), custom_call_target="tpu_custom_call" | custom-call | tf_op jit(solution)/shard_map/lead/pallas_call | solution.py:277
  3.7 0.0 copy-start
  3.7 0.0 copy-start.1
  3.7 0.0 copy-start.2
  3.7 8.6 %all-to-all-start = ((bf16[16,2,16,512]{3,2,1,0:T(8,128)(2,1)}), bf16[16,2,16,512]{3,2,1,0:T(8,128)(2,1)S(1)}, u32[]{:S(2)}, u32[]{:S(2)}) async-start(bf16[16,2,16,512]{3,2,1,0:T(8,128)(2,1)} %get-tuple-element.6), calls=%async_computation | async-start | bytes 1048576 | tf_op jit(solution)/shard_map/all_to_all | solution.py:302
  12.3 1.0 %collective-permute-start = (f32[8,512]{1,0:T(8,128)S(1)}, f32[8,512]{1,0:T(8,128)S(1)}, u32[]{:S(2)}, u32[]{:S(2)}) collective-permute-start(f32[8,512]{1,0:T(8,128)S(1)} %get-tuple-element.7), channel_id=1, source_target_pairs={{0,16},{16,0},{32,48},{48,32},{64,80},{80,64},{96,112},{112,96},{1... | collective-permute-start | bytes 49160 | tf_op jit(solution)/shard_map/ppermute | solution.py:313
  13.3 0.8 %collective-permute-done = f32[8,512]{1,0:T(8,128)S(1)} collective-permute-done((f32[8,512]{1,0:T(8,128)S(1)}, f32[8,512]{1,0:T(8,128)S(1)}, u32[]{:S(2)}, u32[]{:S(2)}) %collective-permute-start) | collective-permute-done | bytes 16416 | tf_op jit(solution)/shard_map/ppermute | solution.py:313
  14.1 2.7 %collective-permute-start.3 = (f32[16,512]{1,0:T(8,128)S(1)}, f32[16,512]{1,0:T(8,128)S(1)}, u32[]{:S(2)}, u32[]{:S(2)}) collective-permute-start(f32[16,512]{1,0:T(8,128)S(1)} %constant_dynamic-update-slice_fusion.refs_0_), channel_id=1, source_target_pairs={{0,96},{16,112},{32,0},{48,16},{64,32},{80,48},{96,64},{112,80},{1... | collective-permute-start | bytes 98312 | tf_op jit(solution)/shard_map/ppermute | solution.py:317
  16.9 0.3 collective-permute-start.2
  17.2 0.7 %collective-permute-start.1 = (f32[16,512]{1,0:T(8,128)S(1)}, f32[16,512]{1,0:T(8,128)S(1)}, u32[]{:S(2)}, u32[]{:S(2)}) collective-permute-start(f32[16,512]{1,0:T(8,128)S(1)} %constant_dynamic-update-slice_fusion.refs_0_), channel_id=1, source_target_pairs={{0,32},{16,48},{32,64},{48,80},{64,96},{80,112},{96,0},{112,16},{1... | collective-permute-start | bytes 98312 | tf_op jit(solution)/shard_map/ppermute | solution.py:317
  17.9 0.0 collective-permute-done.3.refs_3_
  17.9 3.5 %collective-permute-done.2.refs_2_ = f32[16,512]{1,0:T(8,128)S(1)} collective-permute-done((f32[16,512]{1,0:T(8,128)S(1)}, f32[16,512]{1,0:T(8,128)S(1)}, u32[]{:S(2)}, u32[]{:S(2)}) %collective-permute-start.2) | collective-permute-done | bytes 32800 | tf_op jit(solution)/shard_map/ppermute | solution.py:317
  21.4 0.4 collective-permute-done.1.refs_1_
  21.8 0.0 copy-done
  21.8 0.0 copy-done.1
  21.8 0.0 copy-done.2
  21.8 0.3 position_table.1.e_ref
  22.1 0.6 %all-to-all-done = bf16[16,2,16,512]{3,2,1,0:T(8,128)(2,1)S(1)} async-done(((bf16[16,2,16,512]{3,2,1,0:T(8,128)(2,1)}), bf16[16,2,16,512]{3,2,1,0:T(8,128)(2,1)S(1)}, u32[]{:S(2)}, u32[]{:S(2)}) %all-to-all-start) | async-done | bytes 524320 | tf_op jit(solution)/shard_map/all_to_all | solution.py:302
  22.7 3.4 %forward_share.1 = bf16[8,8,2,512]{3,2,1,0:T(2,128)(2,1)S(1)} custom-call(bf16[512,512]{1,0:T(8,128)(2,1)S(1)} %bitcast.2, bf16[8,256,64]{2,1,0:T(8,128)(2,1)S(1)} %copy-done.2, f32[128,512]{1,0:T(8,128)S(1)} %copy-done.1, f32[128,512]{1,0:T(8,128)S(1)} %copy-done, bf16[128,1024]{1,0:T(8,128)(2,1)S(1)} %position_table.1.e_ref, ...), custom_call_target="tpu_custom_call" | custom-call | tf_op jit(solution)/shard_map/forward_share/pallas_call | solution.py:328
  26.1 0.0 copy-start.3
  26.1 11.7 %all_to_all.15.part_ref = bf16[8,8,2,512]{3,2,1,0:T(2,128)(2,1)S(1)} all-to-all(bf16[8,8,2,512]{3,2,1,0:T(2,128)(2,1)S(1)} %forward_share.1), channel_id=1, replica_groups=mesh['facet'=8,'sub'=16] {'facet'}, dimensions={0} | all-to-all | bytes 262144 | tf_op jit(solution)/shard_map/all_to_all | solution.py:344
  37.8 4.3 %backward_share.1 = (f32[2,1,512]{2,1,0:T(1,128)}, bf16[512,512]{1,0:T(8,128)(2,1)S(1)}) custom-call(bf16[8,8,2,512]{3,2,1,0:T(2,128)(2,1)S(1)} %all_to_all.15.part_ref, bf16[128,1024]{1,0:T(8,128)(2,1)S(1)} %position_table.1.e_ref, f32[128,512]{1,0:T(8,128)S(1)} %copy-done.1, f32[128,512]{1,0:T(8,128)S(1)} %copy-done, bf16[8,32,256]{2,1,0:T(8,128)(2,1)S(1)} %copy-done.3, ...), custom_call_target="tpu_custom_call" | custom-call | tf_op jit(solution)/shard_map/backward_share/pallas_call | solution.py:346
  42.1 14.5 %all_to_all.16 = bf16[16,2,16,512]{3,2,1,0:T(8,128)(2,1)S(1)} all-to-all(bf16[16,2,16,512]{3,2,1,0:T(8,128)(2,1)S(1)} %bitcast.3), channel_id=1, replica_groups=mesh['facet'=8,'sub'=16] {'sub'}, dimensions={0} | all-to-all | bytes 1048576 | tf_op jit(solution)/shard_map/all_to_all | solution.py:369
  56.6 0.7 %convert_reduce_fusion = f32[2,16,512]{2,1,0:T(8,128)} fusion(bf16[16,2,16,512]{3,2,1,0:T(8,128)(2,1)S(1)} %all_to_all.16), kind=kLoop, calls=%fused_computation | loop fusion | flops 507904 | bytes 589824 | tf_op jit(solution)/shard_map/reduce_sum | solution.py:370
  (3 shorter events, 0.0 us)
Async XLA Ops:
  3.7 18.1 %copy-start = (f32[128,512]{1,0:T(8,128)S(1)}, f32[128,512]{1,0:T(8,128)}, u32[]{:S(2)}) copy-start(f32[128,512]{1,0:T(8,128)} %constant.13.clone.refs_6_.ts_ref) | copy-start | bytes 786436
  3.7 18.1 %copy-start.1 = (f32[128,512]{1,0:T(8,128)S(1)}, f32[128,512]{1,0:T(8,128)}, u32[]{:S(2)}) copy-start(f32[128,512]{1,0:T(8,128)} %constant.12.clone.refs_5_.tc_ref) | copy-start | bytes 786436
  3.7 18.1 %copy-start.2 = (bf16[8,256,64]{2,1,0:T(8,128)(2,1)S(1)}, bf16[8,256,64]{2,1,0:T(8,128)(2,1)}, u32[]{:S(2)}) copy-start(bf16[8,256,64]{2,1,0:T(8,128)(2,1)} %constant.10.clone.refs_4_.d_ref) | copy-start | bytes 786436
  3.7 19.0 %all-to-all-start = ((bf16[16,2,16,512]{3,2,1,0:T(8,128)(2,1)}), bf16[16,2,16,512]{3,2,1,0:T(8,128)(2,1)S(1)}, u32[]{:S(2)}, u32[]{:S(2)}) async-start(bf16[16,2,16,512]{3,2,1,0:T(8,128)(2,1)} %get-tuple-element.6), calls=%async_computation | async-start | bytes 1048576 | tf_op jit(solution)/shard_map/all_to_all | solution.py:302
  12.3 1.9 %collective-permute-start = (f32[8,512]{1,0:T(8,128)S(1)}, f32[8,512]{1,0:T(8,128)S(1)}, u32[]{:S(2)}, u32[]{:S(2)}) collective-permute-start(f32[8,512]{1,0:T(8,128)S(1)} %get-tuple-element.7), channel_id=1, source_target_pairs={{0,16},{16,0},{32,48},{48,32},{64,80},{80,64},{96,112},{112,96},{1... | collective-permute-start | bytes 49160 | tf_op jit(solution)/shard_map/ppermute | solution.py:313
  14.1 3.8 %collective-permute-start.3 = (f32[16,512]{1,0:T(8,128)S(1)}, f32[16,512]{1,0:T(8,128)S(1)}, u32[]{:S(2)}, u32[]{:S(2)}) collective-permute-start(f32[16,512]{1,0:T(8,128)S(1)} %constant_dynamic-update-slice_fusion.refs_0_), channel_id=1, source_target_pairs={{0,96},{16,112},{32,0},{48,16},{64,32},{80,48},{96,64},{112,80},{1... | collective-permute-start | bytes 98312 | tf_op jit(solution)/shard_map/ppermute | solution.py:317
  16.9 4.6 %collective-permute-start.2 = (f32[16,512]{1,0:T(8,128)S(1)}, f32[16,512]{1,0:T(8,128)S(1)}, u32[]{:S(2)}, u32[]{:S(2)}) collective-permute-start(f32[16,512]{1,0:T(8,128)S(1)} %constant_dynamic-update-slice_fusion.refs_0_), channel_id=1, source_target_pairs={{0,64},{16,80},{32,96},{48,112},{64,0},{80,16},{96,32},{112,48},{1... | collective-permute-start | bytes 98312 | tf_op jit(solution)/shard_map/ppermute | solution.py:317
  17.2 4.6 %collective-permute-start.1 = (f32[16,512]{1,0:T(8,128)S(1)}, f32[16,512]{1,0:T(8,128)S(1)}, u32[]{:S(2)}, u32[]{:S(2)}) collective-permute-start(f32[16,512]{1,0:T(8,128)S(1)} %constant_dynamic-update-slice_fusion.refs_0_), channel_id=1, source_target_pairs={{0,32},{16,48},{32,64},{48,80},{64,96},{80,112},{96,0},{112,16},{1... | collective-permute-start | bytes 98312 | tf_op jit(solution)/shard_map/ppermute | solution.py:317
  26.1 11.7 %copy-start.3 = (bf16[8,32,256]{2,1,0:T(8,128)(2,1)S(1)}, bf16[8,32,256]{2,1,0:T(8,128)(2,1)}, u32[]{:S(2)}) copy-start(bf16[8,32,256]{2,1,0:T(8,128)(2,1)} %constant.11.clone.d_ref) | copy-start | bytes 393220

commit v5 on v4

--- a/solution.py
+++ b/solution.py
@@ -75,24 +75,23 @@
 
 def lead_kernel(
     pos_ref, cnt_ref, y_hbm, u_hbm, v_hbm, obs_hbm, copy_hbm, meta_ref,
-    y_ref, u_ref, v_ref, obs_ref, load_sem, send_sem,
+    u_ref, v_ref, obs_ref, load_sem, send_sem,
 ):
     slots = u_ref.shape[1]
-    pairs = [(y_hbm, y_ref), (u_hbm, u_ref), (v_hbm, v_ref), (obs_hbm, obs_ref)]
+    sends = [
+        pltpu.make_async_copy(y_hbm, copy_hbm.at[n], send_sem.at[n])
+        for n in range(copy_hbm.shape[0])
+    ]
+    for send in sends:
+        send.start()
+    pairs = [(u_hbm, u_ref), (v_hbm, v_ref), (obs_hbm, obs_ref)]
     loads = [
         pltpu.make_async_copy(source, target, load_sem.at[n])
         for n, (source, target) in enumerate(pairs)
     ]
     for load in loads:
         load.start()
-    loads[0].wait()
-    sends = [
-        pltpu.make_async_copy(y_ref, copy_hbm.at[n], send_sem.at[n])
-        for n in range(copy_hbm.shape[0])
-    ]
-    for send in sends:
-        send.start()
-    for load in loads[1:]:
+    for load in loads:
         load.wait()
     meta_ref[0:1, :] = u_ref[...].astype(F32)
     meta_ref[1:2, :] = v_ref[...].astype(F32)
@@ -283,11 +282,10 @@
         in_specs=[smem] * 2 + [hbm] * 4,
         out_specs=(hbm, vmem),
         scratch_shapes=[
-            pltpu.VMEM(facet_data.shape, BF),
             pltpu.VMEM((1, slots), jnp.int32),
             pltpu.VMEM((1, slots), jnp.int32),
             pltpu.VMEM((2, 1, slots), F32),
-            pltpu.SemaphoreType.DMA((4,)),
+            pltpu.SemaphoreType.DMA((3,)),
             pltpu.SemaphoreType.DMA((subs,)),
         ],
         compiler_params=params,

time: 58.3 us -> 73.7 us (1.26)
  Pallas kernels: 9.72 us -> 25.1 us
    pallas_call x1, Pallas kernels: 1.73 us -> 17.2 us  [shards(): pl.pallas_call(lead_kernel, out_shape=(jax.ShapeDtypeStruct((subs,) + fac...]
  transfers between devices with their start and end apart: 5 -> 5, of which waited for: 4 -> 4; matrix products, arithmetic and copies ran while one was open for 0% -> 0% of each run, Pallas kernels for 1% -> 0%
where the time goes in v5:
time: 73.7 us; the launch traced here: 72.7 us
  blocking collectives  26.2 us (36%)
  Pallas kernels  25.1 us (34%)
  starting transfers between devices  13.4 us (18%)
  waiting for transfers between devices  5.29 us (7%)
  between operations  2 us (3%)
    pallas_call x1, Pallas kernels, shards(): pl.pallas_call(lead_kernel, out_shape=(jax.ShapeDtypeStruct((subs,) + fac...  17.2 us
    all_to_all x1, blocking collectives, shards(): image = lax.all_to_all(image, 'sub', 0, 0, tiled=True)  14.5 us
    all_to_all x1, blocking collectives, shards(): parts = lax.all_to_all(part, 'facet', 0, 0, tiled=True)  11.7 us
    all_to_all x1, starting transfers between devices, shards(): gathered = lax.all_to_all(copies, 'sub', 0, 0, tiled=True)  8.56 us
    pallas_call x1, Pallas kernels, shards(): pl.pallas_call(backward_kernel, out_shape=(jax.ShapeDtypeStruct((2, 1, sl...  4.31 us
    ppermute x3, waiting for transfers between devices, shards(): pairs.append(lax.ppermute(pairs[0], 'facet', ring))  3.87 us
    ppermute x3, starting transfers between devices, shards(): pairs.append(lax.ppermute(pairs[0], 'facet', ring))  3.77 us
    pallas_call x1, Pallas kernels, shards(): pl.pallas_call(forward_kernel, out_shape=jax.ShapeDtypeStruct((facets, fa...  3.37 us
  transfers between devices with their start and end apart: 5, of which 4 were waited for; matrix products, arithmetic and copies ran while one was open for 0% of the time, Pallas kernels for 0%

profile of v5, /device:TPU:1, one launch (start us, length us, event | category | flops | bytes accessed | tf_op | source)
XLA Modules:
  0.0 72.7 jit_solution(2752968824025869742)
XLA Ops:
  1.9 17.2 %lead.1 = (bf16[16,2,16,512]{3,2,1,0:T(8,128)(2,1)}, f32[8,512]{1,0:T(8,128)S(1)}) custom-call(s32[1]{0:T(128)S(6)} %copy.13.pos_ref, s32[1]{0:T(128)S(6)} %copy.14.cnt_ref, bf16[2,16,512]{2,1,0:T(8,128)(2,1)} %y_hbm.1, s32[1,512]{1,0:T(1,128)} %u_hbm.1, s32[1,512]{1,0:T(1,128)} %v_hbm.1, f32[2,1,512]{2,1,0:T(1,128)} %obs_hbm.1), custom_call_target="tpu_custom_call" | custom-call | tf_op jit(solution)/shard_map/lead/pallas_call | solution.py:276
  19.1 0.0 copy-start
  19.1 0.0 copy-start.1
  19.1 0.0 copy-start.2
  19.1 8.6 %all-to-all-start = ((bf16[16,2,16,512]{3,2,1,0:T(8,128)(2,1)}), bf16[16,2,16,512]{3,2,1,0:T(8,128)(2,1)S(1)}, u32[]{:S(2)}, u32[]{:S(2)}) async-start(bf16[16,2,16,512]{3,2,1,0:T(8,128)(2,1)} %get-tuple-element.6), calls=%async_computation | async-start | bytes 1048576 | tf_op jit(solution)/shard_map/all_to_all | solution.py:300
  27.7 1.0 %collective-permute-start = (f32[8,512]{1,0:T(8,128)S(1)}, f32[8,512]{1,0:T(8,128)S(1)}, u32[]{:S(2)}, u32[]{:S(2)}) collective-permute-start(f32[8,512]{1,0:T(8,128)S(1)} %get-tuple-element.7), channel_id=1, source_target_pairs={{0,16},{16,0},{32,48},{48,32},{64,80},{80,64},{96,112},{112,96},{1... | collective-permute-start | bytes 49160 | tf_op jit(solution)/shard_map/ppermute | solution.py:311
  28.7 0.8 %collective-permute-done = f32[8,512]{1,0:T(8,128)S(1)} collective-permute-done((f32[8,512]{1,0:T(8,128)S(1)}, f32[8,512]{1,0:T(8,128)S(1)}, u32[]{:S(2)}, u32[]{:S(2)}) %collective-permute-start) | collective-permute-done | bytes 16416 | tf_op jit(solution)/shard_map/ppermute | solution.py:311
  29.6 2.7 %collective-permute-start.3 = (f32[16,512]{1,0:T(8,128)S(1)}, f32[16,512]{1,0:T(8,128)S(1)}, u32[]{:S(2)}, u32[]{:S(2)}) collective-permute-start(f32[16,512]{1,0:T(8,128)S(1)} %constant_dynamic-update-slice_fusion.refs_0_), channel_id=1, source_target_pairs={{0,96},{16,112},{32,0},{48,16},{64,32},{80,48},{96,64},{112,80},{1... | collective-permute-start | bytes 98312 | tf_op jit(solution)/shard_map/ppermute | solution.py:315
  32.3 0.3 collective-permute-start.2
  32.6 0.7 collective-permute-start.1
  33.3 0.0 collective-permute-done.3.refs_3_
  33.3 3.5 %collective-permute-done.2.refs_2_ = f32[16,512]{1,0:T(8,128)S(1)} collective-permute-done((f32[16,512]{1,0:T(8,128)S(1)}, f32[16,512]{1,0:T(8,128)S(1)}, u32[]{:S(2)}, u32[]{:S(2)}) %collective-permute-start.2) | collective-permute-done | bytes 32800 | tf_op jit(solution)/shard_map/ppermute | solution.py:315
  36.9 0.4 collective-permute-done.1.refs_1_
  37.2 0.0 copy-done
  37.2 0.0 copy-done.1
  37.2 0.0 copy-done.2
  37.2 0.3 position_table.1.e_ref
  37.5 0.6 all-to-all-done
  38.1 3.4 %forward_share.1 = bf16[8,8,2,512]{3,2,1,0:T(2,128)(2,1)S(1)} custom-call(bf16[512,512]{1,0:T(8,128)(2,1)S(1)} %bitcast.2, bf16[8,256,64]{2,1,0:T(8,128)(2,1)S(1)} %copy-done.2, f32[128,512]{1,0:T(8,128)S(1)} %copy-done.1, f32[128,512]{1,0:T(8,128)S(1)} %copy-done, bf16[128,1024]{1,0:T(8,128)(2,1)S(1)} %position_table.1.e_ref, ...), custom_call_target="tpu_custom_call" | custom-call | tf_op jit(solution)/shard_map/forward_share/pallas_call | solution.py:326
  41.5 0.0 copy-start.3
  41.5 11.7 %all_to_all.15.part_ref = bf16[8,8,2,512]{3,2,1,0:T(2,128)(2,1)S(1)} all-to-all(bf16[8,8,2,512]{3,2,1,0:T(2,128)(2,1)S(1)} %forward_share.1), channel_id=1, replica_groups=mesh['facet'=8,'sub'=16] {'facet'}, dimensions={0} | all-to-all | bytes 262144 | tf_op jit(solution)/shard_map/all_to_all | solution.py:342
  53.2 4.3 %backward_share.1 = (f32[2,1,512]{2,1,0:T(1,128)}, bf16[512,512]{1,0:T(8,128)(2,1)S(1)}) custom-call(bf16[8,8,2,512]{3,2,1,0:T(2,128)(2,1)S(1)} %all_to_all.15.part_ref, bf16[128,1024]{1,0:T(8,128)(2,1)S(1)} %position_table.1.e_ref, f32[128,512]{1,0:T(8,128)S(1)} %copy-done.1, f32[128,512]{1,0:T(8,128)S(1)} %copy-done, bf16[8,32,256]{2,1,0:T(8,128)(2,1)S(1)} %copy-done.3, ...), custom_call_target="tpu_custom_call" | custom-call | tf_op jit(solution)/shard_map/backward_share/pallas_call | solution.py:344
  57.5 14.5 %all_to_all.16 = bf16[16,2,16,512]{3,2,1,0:T(8,128)(2,1)S(1)} all-to-all(bf16[16,2,16,512]{3,2,1,0:T(8,128)(2,1)S(1)} %bitcast.3), channel_id=1, replica_groups=mesh['facet'=8,'sub'=16] {'sub'}, dimensions={0} | all-to-all | bytes 1048576 | tf_op jit(solution)/shard_map/all_to_all | solution.py:367
  72.0 0.7 convert_reduce_fusion
  (3 shorter events, 0.0 us)
Async XLA Ops:
  19.1 18.1 %copy-start = (f32[128,512]{1,0:T(8,128)S(1)}, f32[128,512]{1,0:T(8,128)}, u32[]{:S(2)}) copy-start(f32[128,512]{1,0:T(8,128)} %constant.13.clone.refs_6_.ts_ref) | copy-start | bytes 786436
  19.1 18.1 %copy-start.1 = (f32[128,512]{1,0:T(8,128)S(1)}, f32[128,512]{1,0:T(8,128)}, u32[]{:S(2)}) copy-start(f32[128,512]{1,0:T(8,128)} %constant.12.clone.refs_5_.tc_ref) | copy-start | bytes 786436
  19.1 18.1 %copy-start.2 = (bf16[8,256,64]{2,1,0:T(8,128)(2,1)S(1)}, bf16[8,256,64]{2,1,0:T(8,128)(2,1)}, u32[]{:S(2)}) copy-start(bf16[8,256,64]{2,1,0:T(8,128)(2,1)} %constant.10.clone.refs_4_.d_ref) | copy-start | bytes 786436
  19.1 19.0 %all-to-all-start = ((bf16[16,2,16,512]{3,2,1,0:T(8,128)(2,1)}), bf16[16,2,16,512]{3,2,1,0:T(8,128)(2,1)S(1)}, u32[]{:S(2)}, u32[]{:S(2)}) async-start(bf16[16,2,16,512]{3,2,1,0:T(8,128)(2,1)} %get-tuple-element.6), calls=%async_computation | async-start | bytes 1048576 | tf_op jit(solution)/shard_map/all_to_all | solution.py:300
  27.7 1.9 %collective-permute-start = (f32[8,512]{1,0:T(8,128)S(1)}, f32[8,512]{1,0:T(8,128)S(1)}, u32[]{:S(2)}, u32[]{:S(2)}) collective-permute-start(f32[8,512]{1,0:T(8,128)S(1)} %get-tuple-element.7), channel_id=1, source_target_pairs={{0,16},{16,0},{32,48},{48,32},{64,80},{80,64},{96,112},{112,96},{1... | collective-permute-start | bytes 49160 | tf_op jit(solution)/shard_map/ppermute | solution.py:311
  29.6 3.8 %collective-permute-start.3 = (f32[16,512]{1,0:T(8,128)S(1)}, f32[16,512]{1,0:T(8,128)S(1)}, u32[]{:S(2)}, u32[]{:S(2)}) collective-permute-start(f32[16,512]{1,0:T(8,128)S(1)} %constant_dynamic-update-slice_fusion.refs_0_), channel_id=1, source_target_pairs={{0,96},{16,112},{32,0},{48,16},{64,32},{80,48},{96,64},{112,80},{1... | collective-permute-start | bytes 98312 | tf_op jit(solution)/shard_map/ppermute | solution.py:315
  32.3 4.6 %collective-permute-start.2 = (f32[16,512]{1,0:T(8,128)S(1)}, f32[16,512]{1,0:T(8,128)S(1)}, u32[]{:S(2)}, u32[]{:S(2)}) collective-permute-start(f32[16,512]{1,0:T(8,128)S(1)} %constant_dynamic-update-slice_fusion.refs_0_), channel_id=1, source_target_pairs={{0,64},{16,80},{32,96},{48,112},{64,0},{80,16},{96,32},{112,48},{1... | collective-permute-start | bytes 98312 | tf_op jit(solution)/shard_map/ppermute | solution.py:315
  32.6 4.6 %collective-permute-start.1 = (f32[16,512]{1,0:T(8,128)S(1)}, f32[16,512]{1,0:T(8,128)S(1)}, u32[]{:S(2)}, u32[]{:S(2)}) collective-permute-start(f32[16,512]{1,0:T(8,128)S(1)} %constant_dynamic-update-slice_fusion.refs_0_), channel_id=1, source_target_pairs={{0,32},{16,48},{32,64},{48,80},{64,96},{80,112},{96,0},{112,16},{1... | collective-permute-start | bytes 98312 | tf_op jit(solution)/shard_map/ppermute | solution.py:315
  41.5 11.7 %copy-start.3 = (bf16[8,32,256]{2,1,0:T(8,128)(2,1)S(1)}, bf16[8,32,256]{2,1,0:T(8,128)(2,1)}, u32[]{:S(2)}) copy-start(bf16[8,32,256]{2,1,0:T(8,128)(2,1)} %constant.11.clone.d_ref) | copy-start | bytes 393220

commit v6 on v4

--- a/solution.py
+++ b/solution.py
@@ -75,7 +75,7 @@
 
 def lead_kernel(
     pos_ref, cnt_ref, y_hbm, u_hbm, v_hbm, obs_hbm, copy_hbm, meta_ref,
-    y_ref, u_ref, v_ref, obs_ref, load_sem, send_sem,
+    y_ref, many_ref, u_ref, v_ref, obs_ref, load_sem, send_sem,
 ):
     slots = u_ref.shape[1]
     pairs = [(y_hbm, y_ref), (u_hbm, u_ref), (v_hbm, v_ref), (obs_hbm, obs_ref)]
@@ -86,9 +86,15 @@
     for load in loads:
         load.start()
     loads[0].wait()
+    block = y_ref[...]
+    repeats = many_ref.shape[0]
+    for n in range(repeats):
+        many_ref[n] = block
     sends = [
-        pltpu.make_async_copy(y_ref, copy_hbm.at[n], send_sem.at[n])
-        for n in range(copy_hbm.shape[0])
+        pltpu.make_async_copy(
+            many_ref, copy_hbm.at[pl.ds(n * repeats, repeats)], send_sem.at[n]
+        )
+        for n in range(copy_hbm.shape[0] // repeats)
     ]
     for send in sends:
         send.start()
@@ -284,11 +290,12 @@
         out_specs=(hbm, vmem),
         scratch_shapes=[
             pltpu.VMEM(facet_data.shape, BF),
+            pltpu.VMEM((subs // 2,) + facet_data.shape, BF),
             pltpu.VMEM((1, slots), jnp.int32),
             pltpu.VMEM((1, slots), jnp.int32),
             pltpu.VMEM((2, 1, slots), F32),
             pltpu.SemaphoreType.DMA((4,)),
-            pltpu.SemaphoreType.DMA((subs,)),
+            pltpu.SemaphoreType.DMA((2,)),
         ],
         compiler_params=params,
         name="lead",

time: 58.3 us -> 58.2 us (level)
  no operation moved by 1% of the time
where the time goes in v6:
time: 58.2 us; the launch traced here: 57.2 us
  blocking collectives  26.2 us (45%)
  starting transfers between devices  13.4 us (23%)
  Pallas kernels  9.61 us (17%)
  waiting for transfers between devices  5.29 us (9%)
  between operations  2 us (3%)
  other arithmetic  0.71 us (1%)
    all_to_all x1, blocking collectives, shards(): image = lax.all_to_all(image, 'sub', 0, 0, tiled=True)  14.5 us
    all_to_all x1, blocking collectives, shards(): parts = lax.all_to_all(part, 'facet', 0, 0, tiled=True)  11.7 us
    all_to_all x1, starting transfers between devices, shards(): gathered = lax.all_to_all(copies, 'sub', 0, 0, tiled=True)  8.56 us
    pallas_call x1, Pallas kernels, shards(): pl.pallas_call(backward_kernel, out_shape=(jax.ShapeDtypeStruct((2, 1, sl...  4.31 us
    ppermute x3, waiting for transfers between devices, shards(): pairs.append(lax.ppermute(pairs[0], 'facet', ring))  3.87 us
    ppermute x3, starting transfers between devices, shards(): pairs.append(lax.ppermute(pairs[0], 'facet', ring))  3.77 us
    pallas_call x1, Pallas kernels, shards(): pl.pallas_call(forward_kernel, out_shape=jax.ShapeDtypeStruct((facets, fa...  3.37 us
    pallas_call x1, Pallas kernels, shards(): pl.pallas_call(lead_kernel, out_shape=(jax.ShapeDtypeStruct((subs,) + fac...  1.63 us
  transfers between devices with their start and end apart: 5, of which 4 were waited for; matrix products, arithmetic and copies ran while one was open for 0% of the time, Pallas kernels for 1%

profile of v6, /device:TPU:1, one launch (start us, length us, event | category | flops | bytes accessed | tf_op | source)
XLA Modules:
  0.0 57.2 jit_solution(13556984848755590428)
XLA Ops:
  1.9 1.6 %lead.1 = (bf16[16,2,16,512]{3,2,1,0:T(8,128)(2,1)}, f32[8,512]{1,0:T(8,128)S(1)}) custom-call(s32[1]{0:T(128)S(6)} %copy.13.pos_ref, s32[1]{0:T(128)S(6)} %copy.14.cnt_ref, bf16[2,16,512]{2,1,0:T(8,128)(2,1)} %y_hbm.1, s32[1,512]{1,0:T(1,128)} %u_hbm.1, s32[1,512]{1,0:T(1,128)} %v_hbm.1, f32[2,1,512]{2,1,0:T(1,128)} %obs_hbm.1), custom_call_target="tpu_custom_call" | custom-call | tf_op jit(solution)/shard_map/lead/pallas_call | solution.py:283
  3.6 0.0 copy-start
  3.6 0.0 copy-start.1
  3.6 0.0 copy-start.2
  3.6 8.6 %all-to-all-start = ((bf16[16,2,16,512]{3,2,1,0:T(8,128)(2,1)}), bf16[16,2,16,512]{3,2,1,0:T(8,128)(2,1)S(1)}, u32[]{:S(2)}, u32[]{:S(2)}) async-start(bf16[16,2,16,512]{3,2,1,0:T(8,128)(2,1)} %get-tuple-element.6), calls=%async_computation | async-start | bytes 1048576 | tf_op jit(solution)/shard_map/all_to_all | solution.py:309
  12.2 1.0 %collective-permute-start = (f32[8,512]{1,0:T(8,128)S(1)}, f32[8,512]{1,0:T(8,128)S(1)}, u32[]{:S(2)}, u32[]{:S(2)}) collective-permute-start(f32[8,512]{1,0:T(8,128)S(1)} %get-tuple-element.7), channel_id=1, source_target_pairs={{0,16},{16,0},{32,48},{48,32},{64,80},{80,64},{96,112},{112,96},{1... | collective-permute-start | bytes 49160 | tf_op jit(solution)/shard_map/ppermute | solution.py:320
  13.2 0.8 %collective-permute-done = f32[8,512]{1,0:T(8,128)S(1)} collective-permute-done((f32[8,512]{1,0:T(8,128)S(1)}, f32[8,512]{1,0:T(8,128)S(1)}, u32[]{:S(2)}, u32[]{:S(2)}) %collective-permute-start) | collective-permute-done | bytes 16416 | tf_op jit(solution)/shard_map/ppermute | solution.py:320
  14.0 2.7 %collective-permute-start.3 = (f32[16,512]{1,0:T(8,128)S(1)}, f32[16,512]{1,0:T(8,128)S(1)}, u32[]{:S(2)}, u32[]{:S(2)}) collective-permute-start(f32[16,512]{1,0:T(8,128)S(1)} %constant_dynamic-update-slice_fusion.refs_0_), channel_id=1, source_target_pairs={{0,96},{16,112},{32,0},{48,16},{64,32},{80,48},{96,64},{112,80},{1... | collective-permute-start | bytes 98312 | tf_op jit(solution)/shard_map/ppermute | solution.py:324
  16.8 0.3 collective-permute-start.2
  17.1 0.7 %collective-permute-start.1 = (f32[16,512]{1,0:T(8,128)S(1)}, f32[16,512]{1,0:T(8,128)S(1)}, u32[]{:S(2)}, u32[]{:S(2)}) collective-permute-start(f32[16,512]{1,0:T(8,128)S(1)} %constant_dynamic-update-slice_fusion.refs_0_), channel_id=1, source_target_pairs={{0,32},{16,48},{32,64},{48,80},{64,96},{80,112},{96,0},{112,16},{1... | collective-permute-start | bytes 98312 | tf_op jit(solution)/shard_map/ppermute | solution.py:324
  17.8 0.0 collective-permute-done.3.refs_3_
  17.8 3.5 %collective-permute-done.2.refs_2_ = f32[16,512]{1,0:T(8,128)S(1)} collective-permute-done((f32[16,512]{1,0:T(8,128)S(1)}, f32[16,512]{1,0:T(8,128)S(1)}, u32[]{:S(2)}, u32[]{:S(2)}) %collective-permute-start.2) | collective-permute-done | bytes 32800 | tf_op jit(solution)/shard_map/ppermute | solution.py:324
  21.3 0.4 collective-permute-done.1.refs_1_
  21.7 0.0 copy-done
  21.7 0.0 copy-done.1
  21.7 0.0 copy-done.2
  21.7 0.3 position_table.1.e_ref
  22.0 0.6 %all-to-all-done = bf16[16,2,16,512]{3,2,1,0:T(8,128)(2,1)S(1)} async-done(((bf16[16,2,16,512]{3,2,1,0:T(8,128)(2,1)}), bf16[16,2,16,512]{3,2,1,0:T(8,128)(2,1)S(1)}, u32[]{:S(2)}, u32[]{:S(2)}) %all-to-all-start) | async-done | bytes 524320 | tf_op jit(solution)/shard_map/all_to_all | solution.py:309
  22.6 3.4 %forward_share.1 = bf16[8,8,2,512]{3,2,1,0:T(2,128)(2,1)S(1)} custom-call(bf16[512,512]{1,0:T(8,128)(2,1)S(1)} %bitcast.2, bf16[8,256,64]{2,1,0:T(8,128)(2,1)S(1)} %copy-done.2, f32[128,512]{1,0:T(8,128)S(1)} %copy-done.1, f32[128,512]{1,0:T(8,128)S(1)} %copy-done, bf16[128,1024]{1,0:T(8,128)(2,1)S(1)} %position_table.1.e_ref, ...), custom_call_target="tpu_custom_call" | custom-call | tf_op jit(solution)/shard_map/forward_share/pallas_call | solution.py:335
  26.0 0.0 copy-start.3
  26.0 11.7 %all_to_all.15.part_ref = bf16[8,8,2,512]{3,2,1,0:T(2,128)(2,1)S(1)} all-to-all(bf16[8,8,2,512]{3,2,1,0:T(2,128)(2,1)S(1)} %forward_share.1), channel_id=1, replica_groups=mesh['facet'=8,'sub'=16] {'facet'}, dimensions={0} | all-to-all | bytes 262144 | tf_op jit(solution)/shard_map/all_to_all | solution.py:351
  37.7 4.3 %backward_share.1 = (f32[2,1,512]{2,1,0:T(1,128)}, bf16[512,512]{1,0:T(8,128)(2,1)S(1)}) custom-call(bf16[8,8,2,512]{3,2,1,0:T(2,128)(2,1)S(1)} %all_to_all.15.part_ref, bf16[128,1024]{1,0:T(8,128)(2,1)S(1)} %position_table.1.e_ref, f32[128,512]{1,0:T(8,128)S(1)} %copy-done.1, f32[128,512]{1,0:T(8,128)S(1)} %copy-done, bf16[8,32,256]{2,1,0:T(8,128)(2,1)S(1)} %copy-done.3, ...), custom_call_target="tpu_custom_call" | custom-call | tf_op jit(solution)/shard_map/backward_share/pallas_call | solution.py:353
  42.0 14.5 %all_to_all.16 = bf16[16,2,16,512]{3,2,1,0:T(8,128)(2,1)S(1)} all-to-all(bf16[16,2,16,512]{3,2,1,0:T(8,128)(2,1)S(1)} %bitcast.3), channel_id=1, replica_groups=mesh['facet'=8,'sub'=16] {'sub'}, dimensions={0} | all-to-all | bytes 1048576 | tf_op jit(solution)/shard_map/all_to_all | solution.py:376
  56.5 0.7 %convert_reduce_fusion = f32[2,16,512]{2,1,0:T(8,128)} fusion(bf16[16,2,16,512]{3,2,1,0:T(8,128)(2,1)S(1)} %all_to_all.16), kind=kLoop, calls=%fused_computation | loop fusion | flops 507904 | bytes 589824 | tf_op jit(solution)/shard_map/reduce_sum | solution.py:377
  (3 shorter events, 0.0 us)
Async XLA Ops:
  3.6 18.1 %copy-start = (f32[128,512]{1,0:T(8,128)S(1)}, f32[128,512]{1,0:T(8,128)}, u32[]{:S(2)}) copy-start(f32[128,512]{1,0:T(8,128)} %constant.13.clone.refs_6_.ts_ref) | copy-start | bytes 786436
  3.6 18.1 %copy-start.1 = (f32[128,512]{1,0:T(8,128)S(1)}, f32[128,512]{1,0:T(8,128)}, u32[]{:S(2)}) copy-start(f32[128,512]{1,0:T(8,128)} %constant.12.clone.refs_5_.tc_ref) | copy-start | bytes 786436
  3.6 18.1 %copy-start.2 = (bf16[8,256,64]{2,1,0:T(8,128)(2,1)S(1)}, bf16[8,256,64]{2,1,0:T(8,128)(2,1)}, u32[]{:S(2)}) copy-start(bf16[8,256,64]{2,1,0:T(8,128)(2,1)} %constant.10.clone.refs_4_.d_ref) | copy-start | bytes 786436
  3.6 19.0 %all-to-all-start = ((bf16[16,2,16,512]{3,2,1,0:T(8,128)(2,1)}), bf16[16,2,16,512]{3,2,1,0:T(8,128)(2,1)S(1)}, u32[]{:S(2)}, u32[]{:S(2)}) async-start(bf16[16,2,16,512]{3,2,1,0:T(8,128)(2,1)} %get-tuple-element.6), calls=%async_computation | async-start | bytes 1048576 | tf_op jit(solution)/shard_map/all_to_all | solution.py:309
  12.2 1.9 %collective-permute-start = (f32[8,512]{1,0:T(8,128)S(1)}, f32[8,512]{1,0:T(8,128)S(1)}, u32[]{:S(2)}, u32[]{:S(2)}) collective-permute-start(f32[8,512]{1,0:T(8,128)S(1)} %get-tuple-element.7), channel_id=1, source_target_pairs={{0,16},{16,0},{32,48},{48,32},{64,80},{80,64},{96,112},{112,96},{1... | collective-permute-start | bytes 49160 | tf_op jit(solution)/shard_map/ppermute | solution.py:320
  14.0 3.8 %collective-permute-start.3 = (f32[16,512]{1,0:T(8,128)S(1)}, f32[16,512]{1,0:T(8,128)S(1)}, u32[]{:S(2)}, u32[]{:S(2)}) collective-permute-start(f32[16,512]{1,0:T(8,128)S(1)} %constant_dynamic-update-slice_fusion.refs_0_), channel_id=1, source_target_pairs={{0,96},{16,112},{32,0},{48,16},{64,32},{80,48},{96,64},{112,80},{1... | collective-permute-start | bytes 98312 | tf_op jit(solution)/shard_map/ppermute | solution.py:324
  16.8 4.6 %collective-permute-start.2 = (f32[16,512]{1,0:T(8,128)S(1)}, f32[16,512]{1,0:T(8,128)S(1)}, u32[]{:S(2)}, u32[]{:S(2)}) collective-permute-start(f32[16,512]{1,0:T(8,128)S(1)} %constant_dynamic-update-slice_fusion.refs_0_), channel_id=1, source_target_pairs={{0,64},{16,80},{32,96},{48,112},{64,0},{80,16},{96,32},{112,48},{1... | collective-permute-start | bytes 98312 | tf_op jit(solution)/shard_map/ppermute | solution.py:324
  17.1 4.6 %collective-permute-start.1 = (f32[16,512]{1,0:T(8,128)S(1)}, f32[16,512]{1,0:T(8,128)S(1)}, u32[]{:S(2)}, u32[]{:S(2)}) collective-permute-start(f32[16,512]{1,0:T(8,128)S(1)} %constant_dynamic-update-slice_fusion.refs_0_), channel_id=1, source_target_pairs={{0,32},{16,48},{32,64},{48,80},{64,96},{80,112},{96,0},{112,16},{1... | collective-permute-start | bytes 98312 | tf_op jit(solution)/shard_map/ppermute | solution.py:324
  26.0 11.7 %copy-start.3 = (bf16[8,32,256]{2,1,0:T(8,128)(2,1)S(1)}, bf16[8,32,256]{2,1,0:T(8,128)(2,1)}, u32[]{:S(2)}) copy-start(bf16[8,32,256]{2,1,0:T(8,128)(2,1)} %constant.11.clone.d_ref) | copy-start | bytes 393220

commit v7 on v6

--- a/solution.py
+++ b/solution.py
@@ -239,17 +239,15 @@
         v = wave * WAVE
         cells = ct_ref[v : v + WAVE, f : f + CHUNK, :].reshape(WAVE * CHUNK, KB * band)
         for n in range(0, SG, RES):
-            cos = tc_ref[f : f + CHUNK, n : n + RES]
-            sin = ts_ref[f : f + CHUNK, n : n + RES]
+            cos = tc_ref[f : f + CHUNK, n : n + RES].astype(BF)
+            sin = ts_ref[f : f + CHUNK, n : n + RES].astype(BF)
             back = dot(cells, e_ref[: KB * band, 2 * n : 2 * (n + RES)], ((1,), (0,)))
-            back = back.reshape(WAVE, CHUNK, 2 * RES)
+            back = back.reshape(WAVE, CHUNK, 2 * RES).astype(BF)
             real_b, imag_b = back[..., :RES], back[..., RES:]
-            m_ref[v : v + WAVE, f : f + CHUNK, n : n + RES] = (
-                real_b * cos - imag_b * sin
-            ).astype(BF)
+            m_ref[v : v + WAVE, f : f + CHUNK, n : n + RES] = real_b * cos - imag_b * sin
             m_ref[v : v + WAVE, RES + f : RES + f + CHUNK, n : n + RES] = (
                 imag_b * cos + real_b * sin
-            ).astype(BF)
+            )
 
     def make_block(v):
         image = dot(d_table, m_ref[v], ((1,), (0,)))

time: 58.2 us -> 58 us (level)
  no operation moved by 1% of the time
where the time goes in v7:
time: 58 us; the launch traced here: 57 us
  blocking collectives  26.2 us (45%)
  starting transfers between devices  13.4 us (23%)
  Pallas kernels  9.39 us (16%)
  waiting for transfers between devices  5.29 us (9%)
  between operations  2 us (3%)
  other arithmetic  0.71 us (1%)
    all_to_all x1, blocking collectives, shards(): image = lax.all_to_all(image, 'sub', 0, 0, tiled=True)  14.5 us
    all_to_all x1, blocking collectives, shards(): parts = lax.all_to_all(part, 'facet', 0, 0, tiled=True)  11.7 us
    all_to_all x1, starting transfers between devices, shards(): gathered = lax.all_to_all(copies, 'sub', 0, 0, tiled=True)  8.56 us
    pallas_call x1, Pallas kernels, shards(): pl.pallas_call(backward_kernel, out_shape=(jax.ShapeDtypeStruct((2, 1, sl...  4.09 us
    ppermute x3, waiting for transfers between devices, shards(): pairs.append(lax.ppermute(pairs[0], 'facet', ring))  3.87 us
    ppermute x3, starting transfers between devices, shards(): pairs.append(lax.ppermute(pairs[0], 'facet', ring))  3.77 us
    pallas_call x1, Pallas kernels, shards(): pl.pallas_call(forward_kernel, out_shape=jax.ShapeDtypeStruct((facets, fa...  3.37 us
    pallas_call x1, Pallas kernels, shards(): pl.pallas_call(lead_kernel, out_shape=(jax.ShapeDtypeStruct((subs,) + fac...  1.63 us
  transfers between devices with their start and end apart: 5, of which 4 were waited for; matrix products, arithmetic and copies ran while one was open for 0% of the time, Pallas kernels for 1%

profile of v7, /device:TPU:1, one launch (start us, length us, event | category | flops | bytes accessed | tf_op | source)
XLA Modules:
  0.0 57.0 jit_solution(341604505736588126)
XLA Ops:
  1.9 1.6 %lead.1 = (bf16[16,2,16,512]{3,2,1,0:T(8,128)(2,1)}, f32[8,512]{1,0:T(8,128)S(1)}) custom-call(s32[1]{0:T(128)S(6)} %copy.13.pos_ref, s32[1]{0:T(128)S(6)} %copy.14.cnt_ref, bf16[2,16,512]{2,1,0:T(8,128)(2,1)} %y_hbm.1, s32[1,512]{1,0:T(1,128)} %u_hbm.1, s32[1,512]{1,0:T(1,128)} %v_hbm.1, f32[2,1,512]{2,1,0:T(1,128)} %obs_hbm.1), custom_call_target="tpu_custom_call" | custom-call | tf_op jit(solution)/shard_map/lead/pallas_call | solution.py:281
  3.6 0.0 copy-start
  3.6 0.0 copy-start.1
  3.6 0.0 copy-start.2
  3.6 8.6 %all-to-all-start = ((bf16[16,2,16,512]{3,2,1,0:T(8,128)(2,1)}), bf16[16,2,16,512]{3,2,1,0:T(8,128)(2,1)S(1)}, u32[]{:S(2)}, u32[]{:S(2)}) async-start(bf16[16,2,16,512]{3,2,1,0:T(8,128)(2,1)} %get-tuple-element.6), calls=%async_computation | async-start | bytes 1048576 | tf_op jit(solution)/shard_map/all_to_all | solution.py:307
  12.2 1.0 %collective-permute-start = (f32[8,512]{1,0:T(8,128)S(1)}, f32[8,512]{1,0:T(8,128)S(1)}, u32[]{:S(2)}, u32[]{:S(2)}) collective-permute-start(f32[8,512]{1,0:T(8,128)S(1)} %get-tuple-element.7), channel_id=1, source_target_pairs={{0,16},{16,0},{32,48},{48,32},{64,80},{80,64},{96,112},{112,96},{1... | collective-permute-start | bytes 49160 | tf_op jit(solution)/shard_map/ppermute | solution.py:318
  13.2 0.8 %collective-permute-done = f32[8,512]{1,0:T(8,128)S(1)} collective-permute-done((f32[8,512]{1,0:T(8,128)S(1)}, f32[8,512]{1,0:T(8,128)S(1)}, u32[]{:S(2)}, u32[]{:S(2)}) %collective-permute-start) | collective-permute-done | bytes 16416 | tf_op jit(solution)/shard_map/ppermute | solution.py:318
  14.0 2.7 %collective-permute-start.3 = (f32[16,512]{1,0:T(8,128)S(1)}, f32[16,512]{1,0:T(8,128)S(1)}, u32[]{:S(2)}, u32[]{:S(2)}) collective-permute-start(f32[16,512]{1,0:T(8,128)S(1)} %constant_dynamic-update-slice_fusion.refs_0_), channel_id=1, source_target_pairs={{0,96},{16,112},{32,0},{48,16},{64,32},{80,48},{96,64},{112,80},{1... | collective-permute-start | bytes 98312 | tf_op jit(solution)/shard_map/ppermute | solution.py:322
  16.8 0.3 collective-permute-start.2
  17.1 0.7 %collective-permute-start.1 = (f32[16,512]{1,0:T(8,128)S(1)}, f32[16,512]{1,0:T(8,128)S(1)}, u32[]{:S(2)}, u32[]{:S(2)}) collective-permute-start(f32[16,512]{1,0:T(8,128)S(1)} %constant_dynamic-update-slice_fusion.refs_0_), channel_id=1, source_target_pairs={{0,32},{16,48},{32,64},{48,80},{64,96},{80,112},{96,0},{112,16},{1... | collective-permute-start | bytes 98312 | tf_op jit(solution)/shard_map/ppermute | solution.py:322
  17.8 0.0 collective-permute-done.3.refs_3_
  17.8 3.5 %collective-permute-done.2.refs_2_ = f32[16,512]{1,0:T(8,128)S(1)} collective-permute-done((f32[16,512]{1,0:T(8,128)S(1)}, f32[16,512]{1,0:T(8,128)S(1)}, u32[]{:S(2)}, u32[]{:S(2)}) %collective-permute-start.2) | collective-permute-done | bytes 32800 | tf_op jit(solution)/shard_map/ppermute | solution.py:322
  21.3 0.4 collective-permute-done.1.refs_1_
  21.7 0.0 copy-done
  21.7 0.0 copy-done.1
  21.7 0.0 copy-done.2
  21.7 0.3 position_table.1.e_ref
  22.0 0.6 %all-to-all-done = bf16[16,2,16,512]{3,2,1,0:T(8,128)(2,1)S(1)} async-done(((bf16[16,2,16,512]{3,2,1,0:T(8,128)(2,1)}), bf16[16,2,16,512]{3,2,1,0:T(8,128)(2,1)S(1)}, u32[]{:S(2)}, u32[]{:S(2)}) %all-to-all-start) | async-done | bytes 524320 | tf_op jit(solution)/shard_map/all_to_all | solution.py:307
  22.6 3.4 %forward_share.1 = bf16[8,8,2,512]{3,2,1,0:T(2,128)(2,1)S(1)} custom-call(bf16[512,512]{1,0:T(8,128)(2,1)S(1)} %bitcast.2, bf16[8,256,64]{2,1,0:T(8,128)(2,1)S(1)} %copy-done.2, f32[128,512]{1,0:T(8,128)S(1)} %copy-done.1, f32[128,512]{1,0:T(8,128)S(1)} %copy-done, bf16[128,1024]{1,0:T(8,128)(2,1)S(1)} %position_table.1.e_ref, ...), custom_call_target="tpu_custom_call" | custom-call | tf_op jit(solution)/shard_map/forward_share/pallas_call | solution.py:333
  26.0 0.0 copy-start.3
  26.0 11.7 %all_to_all.15.part_ref = bf16[8,8,2,512]{3,2,1,0:T(2,128)(2,1)S(1)} all-to-all(bf16[8,8,2,512]{3,2,1,0:T(2,128)(2,1)S(1)} %forward_share.1), channel_id=1, replica_groups=mesh['facet'=8,'sub'=16] {'facet'}, dimensions={0} | all-to-all | bytes 262144 | tf_op jit(solution)/shard_map/all_to_all | solution.py:349
  37.7 4.1 %backward_share.1 = (f32[2,1,512]{2,1,0:T(1,128)}, bf16[512,512]{1,0:T(8,128)(2,1)S(1)}) custom-call(bf16[8,8,2,512]{3,2,1,0:T(2,128)(2,1)S(1)} %all_to_all.15.part_ref, bf16[128,1024]{1,0:T(8,128)(2,1)S(1)} %position_table.1.e_ref, f32[128,512]{1,0:T(8,128)S(1)} %copy-done.1, f32[128,512]{1,0:T(8,128)S(1)} %copy-done, bf16[8,32,256]{2,1,0:T(8,128)(2,1)S(1)} %copy-done.3, ...), custom_call_target="tpu_custom_call" | custom-call | tf_op jit(solution)/shard_map/backward_share/pallas_call | solution.py:351
  41.8 14.5 %all_to_all.16 = bf16[16,2,16,512]{3,2,1,0:T(8,128)(2,1)S(1)} all-to-all(bf16[16,2,16,512]{3,2,1,0:T(8,128)(2,1)S(1)} %bitcast.3), channel_id=1, replica_groups=mesh['facet'=8,'sub'=16] {'sub'}, dimensions={0} | all-to-all | bytes 1048576 | tf_op jit(solution)/shard_map/all_to_all | solution.py:374
  56.3 0.7 %convert_reduce_fusion = f32[2,16,512]{2,1,0:T(8,128)} fusion(bf16[16,2,16,512]{3,2,1,0:T(8,128)(2,1)S(1)} %all_to_all.16), kind=kLoop, calls=%fused_computation | loop fusion | flops 507904 | bytes 589824 | tf_op jit(solution)/shard_map/reduce_sum | solution.py:375
  (3 shorter events, 0.0 us)
Async XLA Ops:
  3.6 18.1 %copy-start = (f32[128,512]{1,0:T(8,128)S(1)}, f32[128,512]{1,0:T(8,128)}, u32[]{:S(2)}) copy-start(f32[128,512]{1,0:T(8,128)} %constant.13.clone.refs_6_.ts_ref) | copy-start | bytes 786436
  3.6 18.1 %copy-start.1 = (f32[128,512]{1,0:T(8,128)S(1)}, f32[128,512]{1,0:T(8,128)}, u32[]{:S(2)}) copy-start(f32[128,512]{1,0:T(8,128)} %constant.12.clone.refs_5_.tc_ref) | copy-start | bytes 786436
  3.6 18.1 %copy-start.2 = (bf16[8,256,64]{2,1,0:T(8,128)(2,1)S(1)}, bf16[8,256,64]{2,1,0:T(8,128)(2,1)}, u32[]{:S(2)}) copy-start(bf16[8,256,64]{2,1,0:T(8,128)(2,1)} %constant.10.clone.refs_4_.d_ref) | copy-start | bytes 786436
  3.6 19.0 %all-to-all-start = ((bf16[16,2,16,512]{3,2,1,0:T(8,128)(2,1)}), bf16[16,2,16,512]{3,2,1,0:T(8,128)(2,1)S(1)}, u32[]{:S(2)}, u32[]{:S(2)}) async-start(bf16[16,2,16,512]{3,2,1,0:T(8,128)(2,1)} %get-tuple-element.6), calls=%async_computation | async-start | bytes 1048576 | tf_op jit(solution)/shard_map/all_to_all | solution.py:307
  12.2 1.9 %collective-permute-start = (f32[8,512]{1,0:T(8,128)S(1)}, f32[8,512]{1,0:T(8,128)S(1)}, u32[]{:S(2)}, u32[]{:S(2)}) collective-permute-start(f32[8,512]{1,0:T(8,128)S(1)} %get-tuple-element.7), channel_id=1, source_target_pairs={{0,16},{16,0},{32,48},{48,32},{64,80},{80,64},{96,112},{112,96},{1... | collective-permute-start | bytes 49160 | tf_op jit(solution)/shard_map/ppermute | solution.py:318
  14.0 3.8 %collective-permute-start.3 = (f32[16,512]{1,0:T(8,128)S(1)}, f32[16,512]{1,0:T(8,128)S(1)}, u32[]{:S(2)}, u32[]{:S(2)}) collective-permute-start(f32[16,512]{1,0:T(8,128)S(1)} %constant_dynamic-update-slice_fusion.refs_0_), channel_id=1, source_target_pairs={{0,96},{16,112},{32,0},{48,16},{64,32},{80,48},{96,64},{112,80},{1... | collective-permute-start | bytes 98312 | tf_op jit(solution)/shard_map/ppermute | solution.py:322
  16.8 4.6 %collective-permute-start.2 = (f32[16,512]{1,0:T(8,128)S(1)}, f32[16,512]{1,0:T(8,128)S(1)}, u32[]{:S(2)}, u32[]{:S(2)}) collective-permute-start(f32[16,512]{1,0:T(8,128)S(1)} %constant_dynamic-update-slice_fusion.refs_0_), channel_id=1, source_target_pairs={{0,64},{16,80},{32,96},{48,112},{64,0},{80,16},{96,32},{112,48},{1... | collective-permute-start | bytes 98312 | tf_op jit(solution)/shard_map/ppermute | solution.py:322
  17.1 4.6 %collective-permute-start.1 = (f32[16,512]{1,0:T(8,128)S(1)}, f32[16,512]{1,0:T(8,128)S(1)}, u32[]{:S(2)}, u32[]{:S(2)}) collective-permute-start(f32[16,512]{1,0:T(8,128)S(1)} %constant_dynamic-update-slice_fusion.refs_0_), channel_id=1, source_target_pairs={{0,32},{16,48},{32,64},{48,80},{64,96},{80,112},{96,0},{112,16},{1... | collective-permute-start | bytes 98312 | tf_op jit(solution)/shard_map/ppermute | solution.py:322
  26.0 11.7 %copy-start.3 = (bf16[8,32,256]{2,1,0:T(8,128)(2,1)S(1)}, bf16[8,32,256]{2,1,0:T(8,128)(2,1)}, u32[]{:S(2)}) copy-start(bf16[8,32,256]{2,1,0:T(8,128)(2,1)} %constant.11.clone.d_ref) | copy-start | bytes 393220
